TPU v7x, 512 devices: a whole 4x8x8 slice. The times are simulated.
512 devices in a mesh: wide: 64 (over y, z), narrow: 8 (over x, core).
Axes of the slice: x: 4, y: 8, z: 8, core: 2. Of those that a mesh axis runs over, the one named last changes fastest.
Arguments:
- hidden: bfloat16 [16384, 1536], P('wide', 'narrow'), may hold values from -6 to 6
- start_state: bfloat16 [1024, 24, 64, 128], P('wide', 'narrow'), may hold values from -0.59765625 to 0.59765625
- tail_inner: bfloat16 [1024, 3, 1536], P('wide', None, 'narrow'), may hold values from -6 to 6
- tail_shared: bfloat16 [1024, 3, 256], P('wide'), may hold values from -6 to 6
- input_gain: float32 [1536], replicated, may hold values from 0.5 to 1.5
- w_gate_inner: bfloat16 [1536, 3072], P(None, 'narrow'), may hold values from -0.15625 to 0.15625
- w_shared: bfloat16 [1536, 256], P(None, 'narrow'), may hold values from -0.15625 to 0.15625
- w_step: bfloat16 [1536, 24], P(None, 'narrow'), may hold values from -0.15625 to 0.15625
- step_bias: float32 [24], P('narrow'), may hold values from -4 to -1
- decay_log: float32 [24], P('narrow'), may hold values from 0 to 2.5
- conv_inner: bfloat16 [4, 1536], P(None, 'narrow'), may hold values from -3 to 3
- conv_inner_bias: float32 [1536], P('narrow'), may hold values from -1.5 to 1.5
- conv_shared: bfloat16 [4, 256], replicated, may hold values from -3 to 3
- conv_shared_bias: float32 [256], replicated, may hold values from -1.5 to 1.5
- skip_gain: float32 [24], P('narrow'), may hold values from 0.5 to 1.5
- gated_gain: float32 [1536], P('narrow'), may hold values from 0.5 to 1.5
- w_output: bfloat16 [1536, 1536], P('narrow'), may hold values from -0.15625 to 0.15625
- next_gain: float32 [1536], replicated, may hold values from 0.5 to 1.5
- w_next: bfloat16 [1536, 3224], P(None, 'narrow'), may hold values from -0.15625 to 0.15625
- dealing: int32 [1024], replicated, may hold values from 0 to 1023, as said below
- accepted: int32 [1024], replicated, may hold values from 0 to 16
- owners: int32 [1024], replicated, may hold values from 0 to 63, as said below
Outputs:
- new_hidden: bfloat16 [16384, 1536], P('wide', 'narrow')
- next_input: bfloat16 [16384, 3224], P('wide', 'narrow')
- kept_state: bfloat16 [1024, 24, 64, 128], P('wide', 'narrow')
- kept_tail_inner: bfloat16 [1024, 3, 1536], P('wide', None, 'narrow')
- kept_tail_shared: bfloat16 [1024, 3, 256], P('wide')
Inputs may be any that keep to these rules, and one draw needn't show every extreme that they name: `dealing`: a permutation of the 1024 requests; slot j lies on index j // 16 of wide. Each owner keeps exactly 16 requests, and the requests of the slots of one index of wide have different owners.
All inputs are finite; a program needn't handle non-finite values.
Results may differ from a plain program's by a relative error of at most 0.02.
Values may be sent and summed in bfloat16 or wider, within the bound.
A program may use at most 64 MiB of HBM per device.

v0:
```python
import jax
import jax.numpy as jnp
from jax import lax
from jax.sharding import PartitionSpec as P

EPSILON = 1e-05
HIGHEST = lax.Precision.HIGHEST


def root_norm(values, gain):
    values = values.astype(jnp.float32)
    factor = lax.rsqrt(jnp.mean(values * values, axis=-1, keepdims=True) + EPSILON)
    return (values * factor * gain).astype(jnp.bfloat16)


def causal_filter(tail, fresh, weight, offset):
    extended = jnp.concatenate([tail, fresh], axis=1)
    length = fresh.shape[1]
    summed = jnp.zeros(fresh.shape, jnp.float32) + offset
    for place in range(weight.shape[0]):
        summed = summed + extended[:, place : place + length].astype(jnp.float32) * weight[
            place
        ].astype(jnp.float32)
    return (jax.nn.silu(summed), extended)


def pick_rows(extended, accepted_now, count):
    length = extended.shape[1]
    wanted = accepted_now[:, None] + jnp.arange(count, dtype=jnp.int32)[None, :]
    onehot = (wanted[:, :, None] == jnp.arange(length, dtype=jnp.int32)[None, None, :]).astype(
        jnp.float32
    )
    return jnp.einsum(
        "rqe,rec->rqc", onehot, extended.astype(jnp.float32), precision=HIGHEST
    ).astype(jnp.bfloat16)


def state_block(
    inner, shared, step_raw, step_bias, decay_log, skip_gain, start_state, accepted_now
):
    states = shared.shape[-1] // 2
    b_part = shared[..., :states]
    c_part = shared[..., states:]
    length = inner.shape[1]
    steps_now = jax.nn.softplus(step_raw.astype(jnp.float32) + step_bias)
    log_decay = steps_now * -jnp.exp(decay_log)
    cumul = jnp.cumsum(log_decay, axis=1)
    prefix = jnp.concatenate([jnp.zeros_like(cumul[:, :1]), cumul], axis=1)
    places = jnp.arange(length, dtype=jnp.int32)
    lower = (places[:, None] >= places[None, :])[None, :, :, None]
    spread = cumul[:, :, None, :] - cumul[:, None, :, :]
    weights = (
        jnp.where(lower, jnp.exp(jnp.where(lower, spread, 0.0)), 0.0) * steps_now[:, None, :, :]
    )
    intersection = jnp.einsum("rtn,rsn->rts", c_part, b_part, precision=HIGHEST)
    mixing = weights * intersection[:, :, :, None]
    state_now = start_state.astype(jnp.float32)
    carried = (
        jnp.einsum("rtn,rhpn->rthp", c_part, state_now, precision=HIGHEST)
        * jnp.exp(cumul)[:, :, :, None]
    )
    direct = jnp.einsum("rtsh,rshp->rthp", mixing, inner, precision=HIGHEST)
    outputs = carried + direct + skip_gain[:, None] * inner
    chosen = (jnp.arange(length + 1, dtype=jnp.int32)[None, :] == accepted_now[:, None]).astype(
        jnp.float32
    )
    ending = jnp.einsum("rk,rkh->rh", chosen, prefix, precision=HIGHEST)
    before = (places[None, :] < accepted_now[:, None])[:, :, None]
    factor = (
        jnp.where(before, jnp.exp(jnp.where(before, ending[:, None, :] - cumul, 0.0)), 0.0)
        * steps_now
    )
    kept = jnp.exp(ending)[:, :, None, None] * state_now + jnp.einsum(
        "rsh,rshp,rsn->rhpn", factor, inner, b_part, precision=HIGHEST
    )
    return (outputs, kept.astype(jnp.bfloat16))


def local(
    hidden,
    start_state,
    tail_inner,
    tail_shared,
    input_gain,
    w_gate_inner,
    w_shared,
    w_step,
    step_bias,
    decay_log,
    conv_inner,
    conv_inner_bias,
    conv_shared,
    conv_shared_bias,
    skip_gain,
    gated_gain,
    w_output,
    next_gain,
    w_next,
    dealing,
    accepted,
    owners,
):
    wide_index = lax.axis_index("wide")
    wide_count = lax.axis_size("wide")
    narrow_count = lax.axis_size("narrow")
    full_rows = lax.all_gather(hidden, "narrow", axis=1, tiled=True)
    normed_in = root_norm(full_rows, input_gain)
    tokens = full_rows.shape[0]
    requests = start_state.shape[0]
    length = tokens // requests
    heads_here = w_step.shape[1]
    head_size = start_state.shape[2]
    block = w_output.shape[0]
    gate_inner = jnp.dot(normed_in, w_gate_inner, preferred_element_type=jnp.float32).astype(
        jnp.bfloat16
    )
    shared_piece = jnp.dot(normed_in, w_shared, preferred_element_type=jnp.float32).astype(
        jnp.bfloat16
    )
    step_raw = jnp.dot(normed_in, w_step, preferred_element_type=jnp.float32).astype(jnp.bfloat16)
    shared_in = lax.all_gather(shared_piece, "narrow", axis=1, tiled=True)
    gate_part = gate_inner[:, :block]
    inner_in = gate_inner[:, block:]
    inner_conv, inner_ext = causal_filter(
        tail_inner, inner_in.reshape(requests, length, block), conv_inner, conv_inner_bias
    )
    shared_conv, shared_ext = causal_filter(
        tail_shared, shared_in.reshape(requests, length, -1), conv_shared, conv_shared_bias
    )
    first_slot = wide_index * requests
    slot_requests = lax.dynamic_slice_in_dim(dealing, first_slot, requests)
    accepted_now = jnp.take(accepted, slot_requests)
    outputs, kept = state_block(
        inner_conv.reshape(requests, length, heads_here, head_size),
        shared_conv,
        step_raw.reshape(requests, length, heads_here),
        step_bias,
        decay_log,
        skip_gain,
        start_state,
        accepted_now,
    )
    gated = outputs.reshape(tokens, block) * jax.nn.silu(gate_part.astype(jnp.float32))
    squares = lax.psum(jnp.sum(gated * gated, axis=1, keepdims=True), "narrow")
    gated_norm = (
        gated * lax.rsqrt(squares / (block * narrow_count) + EPSILON) * gated_gain
    ).astype(jnp.bfloat16)
    partial_sum = jnp.dot(gated_norm, w_output, preferred_element_type=jnp.float32)
    whole_sum = lax.psum(partial_sum.astype(jnp.bfloat16), "narrow").astype(jnp.float32)
    new_full = (full_rows.astype(jnp.float32) + whole_sum).astype(jnp.bfloat16)
    new_part = lax.dynamic_slice_in_dim(
        new_full, lax.axis_index("narrow") * hidden.shape[1], hidden.shape[1], 1
    )
    normed_next = root_norm(new_full, next_gain)
    next_input = jnp.dot(normed_next, w_next, preferred_element_type=jnp.float32).astype(
        jnp.bfloat16
    )
    owner_table = (owners[:, None] == jnp.arange(wide_count, dtype=jnp.int32)[None, :]).astype(
        jnp.int32
    )
    ranking = jnp.sum((jnp.cumsum(owner_table, axis=0) - owner_table) * owner_table, axis=1)
    slot_owner = jnp.take(owners, dealing)
    slot_rank = jnp.take(ranking, dealing)
    local_owner = lax.dynamic_slice_in_dim(slot_owner, first_slot, requests)
    send_table = (jnp.arange(wide_count, dtype=jnp.int32)[:, None] == local_owner[None, :]).astype(
        jnp.bfloat16
    )
    state_bucket = (
        jnp.dot(send_table, kept.reshape(requests, -1), preferred_element_type=jnp.float32)
        .astype(jnp.bfloat16)
        .reshape((wide_count,) + kept.shape[1:])
    )
    inner_edge = pick_rows(inner_ext, accepted_now, tail_inner.shape[1])
    shared_edge = pick_rows(shared_ext, accepted_now, tail_shared.shape[1])
    inner_bucket = jnp.einsum(
        "or,rqc->oqc", send_table, inner_edge, preferred_element_type=jnp.float32
    ).astype(jnp.bfloat16)
    shared_bucket = jnp.einsum(
        "or,rqc->oqc", send_table, shared_edge, preferred_element_type=jnp.float32
    ).astype(jnp.bfloat16)
    state_recv, inner_recv, shared_recv = (
        lax.all_to_all(state_bucket, "wide", split_axis=0, concat_axis=0, tiled=True),
        lax.all_to_all(inner_bucket, "wide", split_axis=0, concat_axis=0, tiled=True),
        lax.all_to_all(shared_bucket, "wide", split_axis=0, concat_axis=0, tiled=True),
    )
    senders = jnp.arange(slot_owner.shape[0], dtype=jnp.int32) // requests
    mine = slot_owner == wide_index
    picking = (
        (slot_rank[:, None] == jnp.arange(requests, dtype=jnp.int32)[None, :]) & mine[:, None]
    ).astype(jnp.bfloat16)
    from_sender = (senders[:, None] == jnp.arange(wide_count, dtype=jnp.int32)[None, :]).astype(
        jnp.bfloat16
    )
    selector = jnp.einsum(
        "jk,jw->kw", picking, from_sender, preferred_element_type=jnp.float32
    ).astype(jnp.bfloat16)
    kept_state = (
        jnp.dot(selector, state_recv.reshape(wide_count, -1), preferred_element_type=jnp.float32)
        .astype(jnp.bfloat16)
        .reshape(start_state.shape)
    )
    kept_tail_inner = jnp.einsum(
        "kw,wqc->kqc", selector, inner_recv, preferred_element_type=jnp.float32
    ).astype(jnp.bfloat16)
    kept_tail_shared = jnp.einsum(
        "kw,wqc->kqc", selector, shared_recv, preferred_element_type=jnp.float32
    ).astype(jnp.bfloat16)
    return (new_part, next_input, kept_state, kept_tail_inner, kept_tail_shared)


def solution(mesh):
    placed = (
        P("wide", "narrow"),
        P("wide", "narrow", None, None),
        P("wide", None, "narrow"),
        P("wide", None, None),
        P(),
        P(None, "narrow"),
        P(None, "narrow"),
        P(None, "narrow"),
        P("narrow"),
        P("narrow"),
        P(None, "narrow"),
        P("narrow"),
        P(),
        P(),
        P("narrow"),
        P("narrow"),
        P("narrow", None),
        P(),
        P(None, "narrow"),
        P(),
        P(),
        P(),
    )
    return jax.shard_map(
        local,
        mesh=mesh,
        in_specs=placed,
        out_specs=(
            P("wide", "narrow"),
            P("wide", "narrow"),
            P("wide", "narrow", None, None),
            P("wide", None, "narrow"),
            P("wide", None, None),
        ),
        check_vma=False,
    )
```

profile of v0, /device:TPU:1, one launch (start us, length us, event | category | flops | bytes accessed | tf_op | source)
XLA Modules:
  0.0 219.3 jit_solution(16669502044702229559)
XLA Ops:
  7.2 0.8 fusion.81
  8.0 0.8 compare_select_fusion.2
  8.8 1.3 gather_fusion
  10.1 0.8 and_select_fusion
  10.9 4.5 %gather_fusion.2 = s32[1024]{0:T(1024)S(1)} fusion(s32[1024]{0:T(1024)S(1)} %copy-done.1, s32[1024]{0:T(1024)S(1)} %fusion.81), kind=kCustom, calls=%fused_computation.1.clone | custom fusion | bytes 12288 | tf_op jit(solution)/shard_map/jit(_take)/gather | solution.py:162
  15.4 0.6 broadcast_compare_fusion
  16.2 20.2 %all_gather.6 = bf16[256,1536]{0,1:T(8,128)(2,1)S(1)} all-gather(bf16[256,192]{0,1:T(8,128)(2,1)S(1)} %copy-done.7), channel_id=1, replica_groups=mesh['wide'=64,'narrow'=8] {'narrow'}, dimensions={1}, use_global_device_ids=true | all-gather | bytes 884736 | tf_op jit(solution)/shard_map/all_gather | solution.py:106
  36.4 0.3 copy.79
  36.7 0.2 fusion.6
  37.0 1.9 convolution_convert_fusion.4
  39.1 0.5 copy-done.6
  39.6 0.2 convolution_convert_fusion.8
  39.8 0.3 convolution_convert_fusion.6
  40.1 0.7 copy.98
  40.9 11.5 %all-to-all-start.1 = ((bf16[64,3,192]{2,1,0:T(4,128)(2,1)}), bf16[64,3,192]{2,1,0:T(4,128)(2,1)}, u32[]{:S(2)}, u32[]{:S(2)}) async-start(bf16[64,3,192]{2,1,0:T(4,128)(2,1)} %copy.98), calls=%async_computation.1 | async-start | bytes 262144 | tf_op jit(solution)/shard_map/all_to_all | solution.py:183
  52.5 0.6 slice_convert_fusion.7
  53.3 0.4 fusion.15
  53.6 0.4 convolution_convert_fusion.11
  54.1 0.1 broadcast_multiply_fusion.1
  54.3 0.2 copy.82
  54.4 0.7 fusion.90
  55.1 0.2 copy.94
  55.7 0.8 copy.95
  56.5 13.0 %all_gather.7 = bf16[256,256]{0,1:T(8,128)(2,1)S(1)} all-gather(bf16[256,32]{0,1:T(8,128)(2,1)S(1)} %convolution_convert_fusion.11), channel_id=1, replica_groups=mesh['wide'=64,'narrow'=8] {'narrow'}, dimensions={1}, use_global_device_ids=true | all-gather | bytes 147456 | tf_op jit(solution)/shard_map/all_gather | solution.py:121
  69.6 0.2 convolution_convert_fusion.7
  69.9 0.3 convolution_convert_fusion.5
  70.2 0.1 copy-done.5
  70.3 0.7 copy.101
  71.0 0.9 divide_multiply_fusion
  72.0 1.1 reshape.238
  73.1 2.2 %broadcast_multiply_fusion = f32[16,16,3,64]{3,2,1,0:T(4,128)} fusion(f32[16,16,3,64]{3,2,1,0:T(4,128)S(1)} %reshape.238, f32[16,16,3]{2,1,0:T(8,128)} %copy.95), kind=kLoop, calls=%fused_computation.72 | loop fusion | flops 49152 | bytes 396288 | tf_op jit(solution)/shard_map/rsh,rshp,rsn->rhpn/dot_general | solution.py:73
  75.3 1.5 divide_multiply_fusion.1
  76.8 12.4 %all-to-all-start.2 = ((bf16[64,3,256]{2,1,0:T(4,128)(2,1)}), bf16[64,3,256]{2,1,0:T(4,128)(2,1)S(1)}, u32[]{:S(2)}, u32[]{:S(2)}) async-start(bf16[64,3,256]{2,1,0:T(4,128)(2,1)} %copy.101), calls=%async_computation.2 | async-start | bytes 262144 | tf_op jit(solution)/shard_map/all_to_all | solution.py:184
  89.2 3.8 %add_convert_fusion = bf16[16,3,64,128]{3,2,1,0:T(8,128)(2,1)S(1)} fusion(bf16[16,3,64,128]{3,2,1,0:T(8,128)(2,1)S(1)} %copy-done.2, f32[16,3]{1,0:T(8,128)S(1)} %copy.93, f32[16,16,3,64]{3,2,1,0:T(4,128)} %broadcast_multiply_fusion, f32[16,16,256]{2,1,0:T(8,128)S(1)} %divide_multiply_fusion.1), kind=kOutput, calls=%fused_computation.21 | convolution fusion | flops 77070336 | bytes 1908736 | tf_op jit(solution)/shard_map/rsh,rshp,rsn->rhpn/dot_general | solution.py:73
  93.0 1.8 fusion.2
  94.8 2.5 %copy.114 = bf16[8,8,192,128]{3,2,1,0:T(8,128)(2,1)} copy(bf16[8,8,192,128]{3,1,2,0:T(8,128)(2,1)S(1)} %fusion.2) | data formatting | bytes 6291456
  97.2 3.4 %all-to-all-done.2 = bf16[64,3,256]{2,1,0:T(4,128)(2,1)S(1)} async-done(((bf16[64,3,256]{2,1,0:T(4,128)(2,1)}), bf16[64,3,256]{2,1,0:T(4,128)(2,1)S(1)}, u32[]{:S(2)}, u32[]{:S(2)}) %all-to-all-start.2) | async-done | bytes 98336 | tf_op jit(solution)/shard_map/all_to_all | solution.py:184
  100.7 9.1 %all-to-all-start = ((bf16[64,3,64,128]{3,2,1,0:T(8,128)(2,1)}), bf16[64,3,64,128]{3,2,1,0:T(8,128)(2,1)}, u32[]{:S(2)}, u32[]{:S(2)}) async-start(bf16[64,3,64,128]{3,2,1,0:T(8,128)(2,1)} %bitcast.87), calls=%async_computation | async-start | bytes 6291456 | tf_op jit(solution)/shard_map/all_to_all | solution.py:182
  109.9 0.6 copy.87
  110.5 0.8 copy.85
  111.3 0.2 copy.83
  111.5 0.3 fusion.59
  111.8 1.7 convolution_multiply_fusion
  113.6 0.6 fusion.14
  114.3 0.2 copy.90
  114.5 0.3 reshape.239
  114.8 1.1 multiply_reduce_fusion
  115.9 13.2 %psum.14 = f32[256,1]{0,1:T(1,128)S(1)} all-reduce(f32[256,1]{0,1:T(1,128)S(1)} %bitcast.96), channel_id=1, replica_groups=mesh['wide'=64,'narrow'=8] {'narrow'}, use_global_device_ids=true, to_apply=%region_3.4 | all-reduce | flops 256 | bytes 2048 | tf_op jit(solution)/shard_map/psum | solution.py:144
  129.1 2.4 %convolution_convert_fusion.2 = bf16[256,1536]{1,0:T(8,128)(2,1)} fusion(bf16[192,1536]{1,0:T(8,128)(2,1)} %param.40, f32[192]{0:T(256)S(1)} %copy-done.24, f32[256]{0:T(256)S(1)} %bitcast.105, f32[256,192]{1,0:T(8,128)S(1)} %reshape.239, bf16[256,384]{1,0:T(8,128)(2,1)} %copy-done.6), kind=kOutput, calls=%fused_computation.7 | convolution fusion | flops 151830528 | bytes 1705728 | tf_op jit(solution)/shard_map/dot_general | solution.py:148
  131.6 18.0 %reduce-window.6 = s32[64,8,128]{2,1,0:T(8,128)S(1)} reduce-window(s32[64,8,128]{2,1,0:T(8,128)S(1)} %fusion.41, s32[]{:T(128)} %constant.71.clone.1), window={size=1x1x128 pad=0_0x0_0x127_0}, to_apply=%region_6.7 | reduce-window | flops 8323072 | bytes 524292 | tf_op jit(solution)/shard_map/reduce-window
  149.6 0.1 slice.102
  149.7 0.1 copy.91
  150.0 0.1 broadcast_add_fusion
  150.2 4.5 %gather_fusion.1 = s32[1024]{0:T(1024)S(1)} fusion(s32[1024]{0:T(1024)S(1)} %fusion.37, s32[1024]{0:T(1024)S(1)} %fusion.81), kind=kCustom, calls=%fused_computation.clone | custom fusion | bytes 12288 | tf_op jit(solution)/shard_map/jit(_take)/gather | solution.py:163
  154.8 0.8 convolution_convert_fusion.12
  155.6 1.7 convolution_convert_fusion.10
  157.2 0.7 convolution_convert_fusion.9
  158.0 46.1 %all-reduce.3.cloned.1.call-done = bf16[256,1536]{1,0:T(8,128)(2,1)} async-done(((bf16[256,1536]{1,0:T(8,128)(2,1)}), bf16[256,1536]{1,0:T(8,128)(2,1)}) %all-reduce.3.cloned.1.call-update) | async-done | bytes 786448 | tf_op jit(solution)/shard_map/psum | solution.py:149
  204.1 1.5 fusion.3
  205.6 0.1 constant_dynamic-slice_fusion
  205.7 0.7 copy.103
  206.4 1.3 convolution_convert_fusion.3
  207.7 3.7 %fusion.10 = bf16[2,8,192,128]{3,1,2,0:T(8,128)(2,1)S(1)} fusion(bf16[16,64]{1,0:T(8,128)(2,1)S(1)} %convolution_convert_fusion.12, bf16[8,8,192,128]{3,2,1,0:T(8,128)(2,1)} %bitcast.34), kind=kOutput, calls=%fused_computation.22 | convolution fusion | flops 50724864 | bytes 3934208 | tf_op jit(solution)/shard_map/dot_general | solution.py:198
  211.4 1.0 copy.116
  (85 shorter events, 1.5 us)
Async XLA Ops:
  7.2 199.3 %copy-start = (bf16[1536,403]{0,1:T(8,128)(2,1)S(1)}, bf16[1536,403]{0,1:T(8,128)(2,1)}, u32[]{:S(2)}) copy-start(bf16[1536,403]{0,1:T(8,128)(2,1)} %param.42) | copy-start | bytes 3714052
  7.2 3.7 %copy-start.1 = (s32[1024]{0:T(1024)S(1)}, s32[1024]{0:T(1024)}, u32[]{:S(2)}) copy-start(s32[1024]{0:T(1024)} %param.45) | copy-start | bytes 12292
  10.9 4.6 %copy-start.12 = (s32[1024]{0:T(1024)S(1)}, s32[1024]{0:T(1024)}, u32[]{:S(2)}) copy-start(s32[1024]{0:T(1024)} %param.43) | copy-start | bytes 12292
  10.9 5.3 %copy-start.10 = (bf16[16,3,192]{2,0,1:T(8,128)(2,1)S(1)}, bf16[16,3,192]{2,0,1:T(8,128)(2,1)}, u32[]{:S(2)}) copy-start(bf16[16,3,192]{2,0,1:T(8,128)(2,1)} %param.26) | copy-start | bytes 55300
  10.9 5.3 %copy-start.7 = (bf16[256,192]{0,1:T(8,128)(2,1)S(1)}, bf16[256,192]{0,1:T(8,128)(2,1)}, u32[]{:S(2)}) copy-start(bf16[256,192]{0,1:T(8,128)(2,1)} %param.24) | copy-start | bytes 294916
  16.1 53.8 %copy-start.15 = (s32[16]{0:T(128)}, s32[16]{0:T(128)S(1)}, u32[]{:S(2)}) copy-start(s32[16]{0:T(128)S(1)} %dynamic_slice.10) | copy-start | bytes 196
  16.2 20.7 %copy-start.22 = (f32[1536]{0:T(1024)S(1)}, f32[1536]{0:T(1024)}, u32[]{:S(2)}) copy-start(f32[1536]{0:T(1024)} %param.28) | copy-start | bytes 18436
  36.9 15.6 %copy-start.25 = (f32[3]{0:T(128)S(1)}, f32[3]{0:T(128)}, u32[]{:S(2)}) copy-start(f32[3]{0:T(128)} %param.33) | copy-start | bytes 40
  36.9 15.6 %copy-start.13 = (bf16[4,192]{1,0:T(4,128)(2,1)S(1)}, bf16[4,192]{1,0:T(4,128)(2,1)}, u32[]{:S(2)}) copy-start(bf16[4,192]{1,0:T(4,128)(2,1)} %param.34) | copy-start | bytes 4612
  37.0 15.6 %copy-start.14 = (bf16[4,256]{1,0:T(4,128)(2,1)S(1)}, bf16[4,256]{1,0:T(4,128)(2,1)}, u32[]{:S(2)}) copy-start(bf16[4,256]{1,0:T(4,128)(2,1)} %param.36) | copy-start | bytes 6148
  37.0 16.3 %copy-start.11 = (bf16[16,3,256]{2,0,1:T(8,128)(2,1)S(1)}, bf16[16,3,256]{2,0,1:T(8,128)(2,1)}, u32[]{:S(2)}) copy-start(bf16[16,3,256]{2,0,1:T(8,128)(2,1)} %param.27) | copy-start | bytes 73732
  37.0 16.3 %copy-start.21 = (bf16[1536,3]{0,1:T(4,128)(2,1)S(1)}, bf16[1536,3]{0,1:T(4,128)(2,1)}, u32[]{:S(2)}) copy-start(bf16[1536,3]{0,1:T(4,128)(2,1)} %param.31) | copy-start | bytes 27652
  38.9 0.7 copy-start.6
  38.9 14.7 %copy-start.20 = (bf16[1536,32]{0,1:T(8,128)(2,1)S(1)}, bf16[1536,32]{0,1:T(8,128)(2,1)}, u32[]{:S(2)}) copy-start(bf16[1536,32]{0,1:T(8,128)(2,1)} %param.30) | copy-start | bytes 294916
  40.9 35.9 %all-to-all-start.1 = ((bf16[64,3,192]{2,1,0:T(4,128)(2,1)}), bf16[64,3,192]{2,1,0:T(4,128)(2,1)}, u32[]{:S(2)}, u32[]{:S(2)}) async-start(bf16[64,3,192]{2,1,0:T(4,128)(2,1)} %copy.98), calls=%async_computation.1 | async-start | bytes 262144 | tf_op jit(solution)/shard_map/all_to_all | solution.py:183
  52.3 1.8 copy-start.19
  53.6 17.4 %copy-start.17 = (f32[192]{0:T(256)S(1)}, f32[192]{0:T(256)}, u32[]{:S(2)}) copy-start(f32[192]{0:T(256)} %param.35) | copy-start | bytes 2308
  69.6 0.7 copy-start.5
  71.0 18.1 %copy-start.2 = (bf16[16,3,64,128]{3,2,1,0:T(8,128)(2,1)S(1)}, bf16[16,3,64,128]{3,2,1,0:T(8,128)(2,1)}, u32[]{:S(2)}) copy-start(bf16[16,3,64,128]{3,2,1,0:T(8,128)(2,1)} %param.25) | copy-start | bytes 2359300
  73.1 2.2 %copy-start.3 = (f32[16,16,3,64]{3,2,1,0:T(4,128)}, f32[16,16,3,64]{3,2,1,0:T(4,128)S(1)}, u32[]{:S(2)}) copy-start(f32[16,16,3,64]{3,2,1,0:T(4,128)S(1)} %reshape.238) | copy-start | bytes 589828
  76.8 23.9 %all-to-all-start.2 = ((bf16[64,3,256]{2,1,0:T(4,128)(2,1)}), bf16[64,3,256]{2,1,0:T(4,128)(2,1)S(1)}, u32[]{:S(2)}, u32[]{:S(2)}) async-start(bf16[64,3,256]{2,1,0:T(4,128)(2,1)} %copy.101), calls=%async_computation.2 | async-start | bytes 262144 | tf_op jit(solution)/shard_map/all_to_all | solution.py:184
  100.7 107.1 %all-to-all-start = ((bf16[64,3,64,128]{3,2,1,0:T(8,128)(2,1)}), bf16[64,3,64,128]{3,2,1,0:T(8,128)(2,1)}, u32[]{:S(2)}, u32[]{:S(2)}) async-start(bf16[64,3,64,128]{3,2,1,0:T(8,128)(2,1)} %bitcast.87), calls=%async_computation | async-start | bytes 6291456 | tf_op jit(solution)/shard_map/all_to_all | solution.py:182
  109.8 3.8 %copy-start.26 = (f32[3]{0:T(128)S(1)}, f32[3]{0:T(128)}, u32[]{:S(2)}) copy-start(f32[3]{0:T(128)} %param.38) | copy-start | bytes 40
  109.8 94.3 %all-reduce.3.cloned.1.call-start = ((), (), s32[]{:S(2)}) async-start(), calls=%async_computation.3 | async-start | bytes 1572864 | tf_op jit(solution)/shard_map/psum | solution.py:149
  111.5 2.1 copy-start.4
  111.5 2.1 copy-start.8
  111.5 2.1 copy-start.9
  113.6 15.5 %copy-start.24 = (f32[192]{0:T(256)S(1)}, f32[192]{0:T(256)}, u32[]{:S(2)}) copy-start(f32[192]{0:T(256)} %param.39) | copy-start | bytes 2308
  150.2 4.6 %copy-start.16 = (pred[1024]{0:T(1024)(128)(4,1)S(1)}, pred[1024]{0:T(1024)(128)(4,1)}, u32[]{:S(2)}) copy-start(pred[1024]{0:T(1024)(128)(4,1)} %get-tuple-element.28) | copy-start | bytes 3076
  150.2 4.6 %copy-start.18 = (pred[1024]{0:T(1024)(128)(4,1)S(1)}, pred[1024]{0:T(1024)(128)(4,1)}, u32[]{:S(2)}) copy-start(pred[1024]{0:T(1024)(128)(4,1)} %get-tuple-element.26) | copy-start | bytes 3076
  155.6 50.9 %copy-start.23 = (f32[1536]{0:T(1024)S(1)}, f32[1536]{0:T(1024)}, u32[]{:S(2)}) copy-start(f32[1536]{0:T(1024)} %param.41) | copy-start | bytes 18436
Sparse Core Ops, SparseCore 0:
  131.7 72.3 all-reduce.2
where the time goes:
time: 220 us; the launch traced here: 219 us
  waiting for transfers between devices  49.5 us (22%)
  blocking collectives  46.4 us (21%)
  starting transfers between devices  33 us (15%)
  other arithmetic  30.4 us (14%)
  local copies, waits for them, and re-layouts  22.8 us (10%)
  matrix products  22.6 us (10%)
  between operations  14.6 us (7%)
    psum x1, waiting for transfers between devices, local(): lax.psum(partial_sum.astype(jnp.bfloat16), 'narrow').astype(jnp.float32)  46.1 us
    all_gather x1, blocking collectives, local(): full_rows = lax.all_gather(hidden, 'narrow', axis=1, tiled=True)  20.2 us
    another operation x3, other arithmetic  18.2 us
    psum x1, blocking collectives, local(): squares = lax.psum(jnp.sum(gated * gated, axis=1, keepdims=True), 'narrow')  13.2 us
    all_gather x1, blocking collectives, local(): shared_in = lax.all_gather(shared_piece, 'narrow', axis=1, tiled=True)  13 us
    all_to_all x1, starting transfers between devices, local(): lax.all_to_all(shared_bucket, 'wide', split_axis=0, concat_axis=0, tiled=...  12.4 us
    all_to_all x1, starting transfers between devices, local(): lax.all_to_all(inner_bucket, 'wide', split_axis=0, concat_axis=0, tiled=T...  11.5 us
    all_to_all x1, starting transfers between devices, local(): lax.all_to_all(state_bucket, 'wide', split_axis=0, concat_axis=0, tiled=T...  9.12 us
  transfers between devices with their start and end apart: 4, of which 2 were waited for; matrix products, arithmetic and copies ran while one was open for 26% of the time, Pallas kernels for 0%

commit v1 on v0

v1 whole, which is shorter than its diff:
```python
import functools

import jax
import jax.numpy as jnp
from jax import lax
from jax.experimental import pallas as pl
from jax.experimental.pallas import tpu as pltpu
from jax.sharding import PartitionSpec as P

EPSILON = 1e-05
HIGHEST = lax.Precision.HIGHEST
MESH = pl.DeviceIdType.MESH
F32 = jnp.float32
BF16 = jnp.bfloat16


def fdot(a, b):
    return jnp.dot(a, b, precision=HIGHEST, preferred_element_type=F32)


def bdot(a, b):
    return jnp.dot(a, b, preferred_element_type=F32)


SIDE = 8
FAR = 4
BASE = (0, 0, 16, 32, 44)
STEPS = (4, 12, 16, 16)


def hop_base(dist):
    return jnp.where(dist <= 1, 0, jnp.where(dist == 2, 16, jnp.where(dist == 3, 32, 44)))


def table_values(dealing, owners, accepted, me, per=16):
    T = dealing.shape[1]
    ln = lax.broadcasted_iota(jnp.int32, (1, T), 1)
    sub = lax.broadcasted_iota(jnp.int32, (T, T), 0)
    pick = (sub == dealing).astype(BF16)
    row8 = lax.broadcasted_iota(jnp.int32, (8, T), 0)
    known = jnp.where(row8 == 0, owners, accepted).astype(F32).astype(BF16)
    per_slot = jnp.dot(known, pick, preferred_element_type=F32).astype(jnp.int32)
    owner = per_slot[0:1]
    acc = per_slot[1:2]
    sender = ln >> 4
    ys, zs = sender >> 3, sender & 7
    yo, zo = owner >> 3, owner & 7
    me_y, me_z = me // SIDE, lax.rem(me, SIDE)
    halves = []
    keys, starts = [], []
    for fs, fo, gs, go in ((zs, zo, ys, yo), (ys, yo, zs, zo)):
        d1 = (fo - fs) & 7
        back1 = jnp.where((d1 > FAR) | ((d1 == FAR) & ((go & 1) == 1)), 1, 0)
        dist1 = jnp.where(back1 == 1, SIDE - d1, d1)
        d2 = (go - gs) & 7
        back2 = jnp.where((d2 > FAR) | ((d2 == FAR) & ((fs & 1) == 1)), 1, 0)
        dist2 = jnp.where(back2 == 1, SIDE - d2, d2)
        for group, dist in ((sender * 2 + back1, dist1), (owner * 2 + back2, dist2)):
            start = group * (8 * T)
            starts.append(start.astype(F32))
            keys.append((start + (FAR - dist) * T + ln).astype(F32))
        halves.append((back1, dist1, back2, dist2))
    starts.append((owner * T).astype(F32))
    keys.append((owner * T + dealing).astype(F32))
    stacked = jnp.where(row8 == 0, keys[0], jnp.where(row8 == 1, keys[1], jnp.where(row8 == 2, keys[2], jnp.where(row8 == 3, keys[3], keys[4]))))
    return ln, sender, owner, acc, me_y, me_z, halves, keys, starts, stacked


def finish_tables(ln, sender, owner, acc, me, halves, places):
    T = ln.shape[1]
    lane = lax.broadcasted_iota(jnp.int32, (128, 128), 1)
    sub = lax.broadcasted_iota(jnp.int32, (128, 128), 0)
    t = lax.broadcasted_iota(jnp.int32, (128, 1), 0)
    def to_row(column):
        return jnp.sum(jnp.where(lane == sub, column.astype(F32), 0.0), axis=0, keepdims=True).astype(jnp.int32)
    def lookup(want, key, value, missing):
        return to_row(jnp.max(jnp.where(want == key, value, missing).astype(F32), axis=1, keepdims=True))
    me_y, me_z = me // SIDE, lax.rem(me, SIDE)
    out = []
    for h in (0, 1):
        back1, dist1, back2, dist2 = halves[h]
        pos1, pos2 = places[2 * h], places[2 * h + 1]
        loc = jnp.where(dist1 == 0, ln & 15, 16 + back1 * 48 + hop_base(dist1) + pos1)
        out.append(lookup(me * 32 + t, sender * 32 + back1 * 16 + pos1, ln & 15, 0))
        back_t = jnp.where(t >= 48, 1, 0)
        q = t - 48 * back_t
        hop = jnp.where(q < 4, 4, jnp.where(q < 16, 3, jnp.where(q < 32, 2, 1)))
        i = q - jnp.where(q < 4, 0, jnp.where(q < 16, 4, jnp.where(q < 32, 16, 32)))
        move = jnp.where(back_t == 1, -hop, hop)
        if h == 0:
            dest = ((me_y + move) & 7) * SIDE + me_z
        else:
            dest = me_y * SIDE + ((me_z + move) & 7)
        out.append(lookup(((dest * 2 + back_t) * 8 + hop) * 16 + i, ((owner * 2 + back2) * 8 + dist2) * 16 + pos2, loc, -1))
        out.append(lookup(me * 16 + t, owner * 16 + places[4], jnp.where(dist2 == 0, loc, 128 + back2 * 16 + pos2), 0))
    out.append(lookup(me * 16 + t, ln, acc, 0))
    out.append(out[-1])
    r = lax.broadcasted_iota(jnp.int32, (8, 128), 0)
    table = jnp.zeros((8, 128), jnp.int32)
    for k in range(7):
        table = jnp.where(r == k, out[k], table)
    return table


def table_kernel(dealing_ref, owners_ref, accepted_ref, table_ref, count_ref, columns):
    me = lax.axis_index("wide")
    ln, sender, owner, acc, me_y, me_z, halves, keys, starts, stacked = table_values(
        dealing_ref[...], owners_ref[...], accepted_ref[...], me
    )
    columns[...] = jnp.transpose(stacked)
    total = ln.shape[1]
    chunk = 64

    def count(step, found):
        part = columns[pl.ds(pl.multiple_of(step * chunk, chunk), chunk), :]
        return tuple(
            found[k]
            + jnp.sum(
                jnp.where((part[:, k : k + 1] >= starts[k]) & (part[:, k : k + 1] < keys[k]), 1.0, 0.0),
                axis=0,
                keepdims=True,
            )
            for k in range(5)
        )

    found = lax.fori_loop(
        0, total // chunk, count, tuple(jnp.zeros((1, total), F32) for _ in range(5))
    )
    table_ref[...] = finish_tables(
        ln, sender, owner, acc, me, halves, [places.astype(jnp.int32) for places in found]
    )
    tokens = count_ref.shape[0]
    slot = lax.broadcasted_iota(jnp.int32, (tokens, total), 0) >> 4
    at = lax.broadcasted_iota(jnp.int32, (tokens, total), 1)
    count_ref[...] = jnp.sum(
        jnp.where(at == me * 16 + slot, acc, 0).astype(F32), axis=1, keepdims=True
    ).astype(jnp.int32)


CAPS = (16, 16, 12, 4)
OFFS = (0, 16, 32, 44)
SECOND_OFFS = (0, 4, 16, 32)


class Route:
    def __init__(self, number, table, refs, send_sem, recv_sem, side):
        self.number, self.table, self.send_sem, self.recv_sem, self.side = (
            number, table, send_sem, recv_sem, side
        )
        self.pool, self.lists, self.passing, self.final, self.second = refs

    def neighbour(self, half, back, phase):
        me = lax.axis_index("wide")
        side = self.side
        y, z = me // side, lax.rem(me, side)
        move = side - 1 if back else 1
        if (half == 0) == (phase == 0):
            return y * side + lax.rem(z + move, side)
        return lax.rem(y + move, side) * side + z

    def copy(self, phase, half, back, hop):
        if phase == 0:
            low = 16 + 48 * back
            if hop == 0:
                source = self.lists.at[half, back]
            else:
                source = self.pool.at[half, pl.ds(low + OFFS[hop - 1], CAPS[hop])]
            target = self.pool.at[half, pl.ds(low + OFFS[hop], CAPS[hop])]
        else:
            size = CAPS[3 - hop]
            source = self.second.at[half, back, pl.ds(SECOND_OFFS[hop], size)]
            if hop < 3:
                target = self.passing.at[half, back, pl.ds(SECOND_OFFS[hop], size)]
            else:
                target = self.final.at[half, pl.ds(16 * back, size)]
        at = (((self.number * 2 + phase) * 2 + half) * 2 + back) * 4 + hop
        return pltpu.make_async_remote_copy(
            src_ref=source,
            dst_ref=target,
            send_sem=self.send_sem.at[at],
            recv_sem=self.recv_sem.at[at],
            device_id={"wide": self.neighbour(half, back, phase)},
            device_id_type=MESH,
        )

    def each(self, phase, hop):
        return [self.copy(phase, half, back, hop) for half in (0, 1) for back in (0, 1)]

    def fill(self, blocks, rows):
        for half in (0, 1):
            low = half * rows

            def own(i, carry):
                self.pool[half, i] = blocks[i, low : low + rows, :]
                return carry

            lax.fori_loop(0, 16, own, 0)
            for back in (0, 1):

                def listed(i, carry):
                    self.lists[half, back, i] = blocks[self.table[3 * half, 16 * back + i], low : low + rows, :]
                    return carry

                lax.fori_loop(0, 16, listed, 0)

    def first(self, hop):
        if hop > 0:
            for copy in self.each(0, hop - 1):
                copy.wait_recv()
        if hop < 4:
            for copy in self.each(0, hop):
                copy.start()

    def after(self, hop):
        if hop > 0:
            for copy in self.each(1, hop - 1):
                copy.wait_recv()
        if hop == 4:
            return
        low = SECOND_OFFS[hop]
        size = CAPS[3 - hop]
        known = CAPS[4 - hop] if hop > 0 else 0
        for half in (0, 1):
            for back in (0, 1):

                def merged(i, carry):
                    at = self.table[3 * half + 1, 48 * back + low + i]
                    mine = self.pool[half, jnp.maximum(at, 0)]
                    came = self.passing[half, back, SECOND_OFFS[hop - 1] + i]
                    self.second[half, back, low + i] = jnp.where(at >= 0, mine, came)
                    return carry

                def fresh(i, carry):
                    at = self.table[3 * half + 1, 48 * back + low + i]
                    self.second[half, back, low + i] = self.pool[half, jnp.maximum(at, 0)]
                    return carry

                if known:
                    lax.fori_loop(0, known, merged, 0)
                if known < size:
                    lax.fori_loop(known, size, fresh, 0)
        for copy in self.each(1, hop):
            copy.start()

    def collect(self, blocks, rows):
        for half in (0, 1):
            low = half * rows

            def take(k, carry):
                at = self.table[3 * half + 2, k]
                here = self.pool[half, jnp.where(at < 128, at, 0)]
                came = self.final[half, jnp.where(at < 128, 0, at - 128)]
                blocks[k, low : low + rows, :] = jnp.where(at < 128, here, came)
                return carry

            lax.fori_loop(0, 16, take, 0)

    def drain(self):
        for phase in (0, 1):
            for hop in range(4):
                for copy in self.each(phase, hop):
                    copy.wait_send()


def layer_kernel(
    count,
    side,
    table_ref,
    acc_ref,
    hidden_ref,
    start_ref,
    tail_inner_ref,
    tail_shared_ref,
    gain_ref,
    w_gate_ref,
    w_inner_ref,
    w_small_ref,
    bias_ref,
    decay_ref,
    conv_inner_ref,
    conv_inner_bias_ref,
    conv_shared_ref,
    conv_shared_bias_ref,
    skip_ref,
    gated_gain_ref,
    w_out_ref,
    next_gain_ref,
    w_next_ref,
    new_ref,
    next_ref,
    kept_ref,
    kept_inner_ref,
    kept_shared_ref,
    gather_buf,
    small_out,
    small_buf,
    square_out,
    square_buf,
    part_out,
    part_buf,
    new_buf,
    message,
    state_out,
    state_pool,
    state_lists,
    state_passing,
    state_final,
    state_second,
    news_pool,
    news_lists,
    news_passing,
    news_final,
    news_second,
    send_sem,
    recv_sem,
    route_send,
    route_recv,
):
    me = lax.axis_index("narrow")
    states = Route(
        0,
        table_ref,
        (state_pool, state_lists, state_passing, state_final, state_second),
        route_send,
        route_recv,
        side,
    )
    updates = Route(
        1,
        table_ref,
        (news_pool, news_lists, news_passing, news_final, news_second),
        route_send,
        route_recv,
        side,
    )
    tokens, block = hidden_ref.shape
    requests = start_ref.shape[0]
    length = tokens // requests
    width = block * count
    barrier = pltpu.get_barrier_semaphore()
    for step in range(1, count):
        pl.semaphore_signal(
            barrier, inc=1, device_id={"narrow": lax.rem(me + step, count)}, device_id_type=MESH
        )
    for half in (0, 1):
        for back in (0, 1):
            pl.semaphore_signal(
                barrier,
                inc=1,
                device_id={"wide": states.neighbour(half, back, 0)},
                device_id_type=MESH,
            )
    pl.semaphore_wait(barrier, count + 3)

    def send(source, target_buf, stage, step):
        pltpu.make_async_remote_copy(
            src_ref=source,
            dst_ref=target_buf.at[me],
            send_sem=send_sem.at[stage],
            recv_sem=recv_sem.at[stage],
            device_id={"narrow": lax.rem(me + step, count)},
            device_id_type=MESH,
        ).start()

    def finish(target_buf, stage):
        some = target_buf.at[pl.ds(0, count - 1)]
        both = pltpu.make_async_remote_copy(
            src_ref=some,
            dst_ref=some,
            send_sem=send_sem.at[stage],
            recv_sem=recv_sem.at[stage],
            device_id={"narrow": lax.rem(me + 1, count)},
            device_id_type=MESH,
        )
        both.wait_recv()
        both.wait_send()

    for step in range(1, count):
        send(hidden_ref, gather_buf, 0, step)
    gather_buf[me] = hidden_ref[...]
    half_rows = start_ref.shape[1] // 2
    states.fill(start_ref, half_rows)
    states.first(0)

    rows = lax.broadcasted_iota(jnp.int32, (tokens, tokens), 0)
    cols = lax.broadcasted_iota(jnp.int32, (tokens, tokens), 1)
    same = (rows >> 4) == (cols >> 4)
    tri = same & (cols <= rows)
    eye = rows == cols
    place = rows[:, :1] & (length - 1)
    acc = acc_ref[...]
    lane = lax.broadcasted_iota(jnp.int32, (tokens, block), 1)

    def to_row(column):
        return jnp.sum(jnp.where(eye, column, 0.0), axis=0, keepdims=True)

    def to_column(row):
        return jnp.sum(jnp.where(eye, row, 0.0), axis=1, keepdims=True)

    def spread(values):
        return jnp.where(
            lane < 64, values[:, 0:1], jnp.where(lane < 128, values[:, 1:2], values[:, 2:3])
        )

    def normed(buf, gains):
        total = jnp.zeros((tokens, 1), F32)
        for n in range(count):
            piece = buf[n].astype(F32)
            total = total + jnp.sum(piece * piece, axis=1, keepdims=True)
        factor = lax.rsqrt(total / width + EPSILON)
        return [(buf[n].astype(F32) * factor * gains[n]).astype(BF16) for n in range(count)]

    states.first(1)
    finish(gather_buf, 0)
    gate = jnp.zeros((tokens, block), F32)
    inner = jnp.zeros((tokens, block), F32)
    small = jnp.zeros((tokens, 128), F32)
    pieces = normed(gather_buf, gain_ref)
    for n in range(count):
        small = small + bdot(pieces[n], w_small_ref[n])
    small_out[...] = small.astype(BF16)
    for step in range(1, count):
        send(small_out, small_buf, 1, step)
    small_buf[me] = small_out[...]
    for n in range(count):
        inner = inner + bdot(pieces[n], w_inner_ref[n])
        gate = gate + bdot(pieces[n], w_gate_ref[n])
    gate = gate.astype(BF16).astype(F32)
    states.first(2)
    inner_bf = inner.astype(BF16)

    def filtered(fresh, tail, weight, offset):
        total = offset + fresh * weight[3:4]
        for shift in (1, 2, 3):
            moved = jnp.where(
                place >= shift,
                pltpu.roll(fresh, shift, 0),
                pltpu.roll(tail, tokens - length + shift, 0),
            )
            total = total + moved * weight[3 - shift : 4 - shift]
        return jax.nn.silu(total)

    tail_inner = tail_inner_ref[...]
    tail_shared = tail_shared_ref[...]
    conv_i = filtered(
        inner_bf.astype(F32),
        tail_inner.astype(F32),
        conv_inner_ref[...].astype(F32),
        conv_inner_bias_ref[...],
    )

    raw = small.astype(BF16).astype(F32) + bias_ref[...]
    steps = jnp.maximum(raw, 0.0) + jnp.log1p(jnp.exp(-jnp.abs(raw)))
    log_decay = steps * -jnp.exp(decay_ref[...])
    cumul = fdot(tri.astype(F32), log_decay)
    col_place = cols & (length - 1)
    ending = fdot((same & (col_place < acc)).astype(F32), log_decay)
    before = place < acc
    factor = jnp.where(before, jnp.exp(jnp.where(before, ending - cumul, 0.0)), 0.0) * steps
    decayed = jnp.exp(ending)
    weighted = (conv_i * spread(factor)).astype(BF16)

    states.first(3)
    finish(small_buf, 1)
    lane_in = lax.broadcasted_iota(jnp.int32, (128, 256), 0)
    lane_out = lax.broadcasted_iota(jnp.int32, (128, 256), 1)
    shared = jnp.zeros((tokens, 256), F32)
    for n in range(count):
        pick = (lane_in >= 32) & (lane_in < 64) & (lane_out == lane_in - 32 + 32 * n)
        shared = shared + bdot(small_buf[n], pick.astype(BF16))
    conv_s = filtered(
        shared, tail_shared.astype(F32), conv_shared_ref[...].astype(F32), conv_shared_bias_ref[...]
    )
    b_part = conv_s[:, :128]
    c_part = conv_s[:, 128:]

    edge = rows[:, :1] & 15
    wanted = jnp.where(
        edge < 3, edge, jnp.where(edge < 6, edge - 3, jnp.where(edge < 9, edge - 6, edge - 9))
    )
    target = acc + wanted - 3
    sel_fresh = (same & (col_place == target)).astype(BF16)
    sel_tail = (same & (col_place == target + length)).astype(BF16)
    edge_i = bdot(sel_fresh, inner_bf) + bdot(sel_tail, tail_inner)
    edge_s = bdot(sel_fresh, shared.astype(BF16)) + bdot(sel_tail, tail_shared)
    pick_in = lax.broadcasted_iota(jnp.int32, (block, 128), 0)
    pick_out = lax.broadcasted_iota(jnp.int32, (block, 128), 1)
    last_head = (pick_in == pick_out + 128).astype(BF16)
    high = decayed.astype(BF16).astype(F32)
    low = decayed - high
    edges = jnp.where(
        edge < 3,
        edge_i[:, :128],
        jnp.where(
            edge < 6,
            bdot(edge_i.astype(BF16), last_head),
            jnp.where(
                edge < 9,
                edge_s[:, :128],
                jnp.where(
                    edge < 12, edge_s[:, 128:], jnp.where(edge == 12, high, jnp.where(edge == 13, low, 0.0))
                ),
            ),
        ),
    )
    message[:, 0:16, :] = weighted[:, :128].reshape(requests, length, 128)
    message[:, 16:32, :] = bdot(weighted, last_head).astype(BF16).reshape(requests, length, 128)
    message[:, 32:48, :] = b_part.astype(BF16).reshape(requests, length, 128)
    message[:, 48:64, :] = edges.astype(BF16).reshape(requests, length, 128)

    updates.fill(message, 32)
    updates.first(0)
    states.first(4)
    states.after(0)

    crossing = lax.dot_general(
        c_part, b_part, (((1,), (1,)), ((), ())), precision=HIGHEST, preferred_element_type=F32
    )
    direct = jnp.zeros((tokens, block), F32)
    for head in range(3):
        column = cumul[:, head : head + 1]
        gap = jnp.where(tri, column - to_row(column), 0.0)
        mixing = jnp.where(tri, jnp.exp(gap), 0.0) * to_row(steps[:, head : head + 1]) * crossing
        direct = direct + fdot(mixing, jnp.where((lane >> 6) == head, conv_i, 0.0))
    updates.first(1)
    states.after(1)
    carried = lax.dot_general(
        c_part.reshape(requests, length, 128),
        start_ref[...].astype(F32),
        (((2,), (2,)), ((0,), (0,))),
        precision=HIGHEST,
        preferred_element_type=F32,
    ).reshape(tokens, block)
    outputs = carried * spread(jnp.exp(cumul)) + direct + skip_ref[...] * conv_i
    gated = outputs * jax.nn.silu(gate)
    square_out[...] = lax.dot_general(
        jnp.ones((8, block), F32),
        gated * gated,
        (((1,), (1,)), ((), ())),
        precision=HIGHEST,
        preferred_element_type=F32,
    )
    for step in range(1, count):
        send(square_out, square_buf, 2, step)
    square_buf[me] = square_out[...]
    scaled = (gated * gated_gain_ref[...]).astype(BF16)
    for step in range(1, count):
        towards = lax.rem(me + step, count)
        part_out[towards] = bdot(scaled, w_out_ref[towards]).astype(BF16)
        send(part_out.at[towards], part_buf, 3, step)
    part_buf[me] = bdot(scaled, w_out_ref[me]).astype(BF16)

    updates.first(2)
    states.after(2)
    finish(square_buf, 2)
    squares = square_buf[0]
    for n in range(1, count):
        squares = squares + square_buf[n]
    factor_out = lax.rsqrt(to_column(squares[0:1]) / width + EPSILON)
    finish(part_buf, 3)
    summed = part_buf[0].astype(F32)
    for n in range(1, count):
        summed = summed + part_buf[n].astype(F32)
    new_ref[...] = (hidden_ref[...].astype(F32) + summed * factor_out).astype(BF16)
    for step in range(1, count):
        send(new_ref, new_buf, 4, step)
    new_buf[me] = new_ref[...]
    updates.first(3)
    states.after(3)
    finish(new_buf, 4)
    pieces = normed(new_buf, next_gain_ref)
    projected = jnp.zeros(next_ref.shape, F32)
    for n in range(count):
        projected = projected + bdot(pieces[n], w_next_ref[n])
    next_ref[...] = projected.astype(BF16)
    updates.first(4)
    updates.after(0)
    updates.after(1)
    updates.after(2)
    updates.after(3)
    states.after(4)
    updates.after(4)
    states.drain()
    updates.drain()
    states.collect(state_out, half_rows)
    updates.collect(message, 32)
    over = (((1,), (1,)), ((0,), (0,)))
    b_rows = message[:, 32:48, :]
    first = lax.dot_general(message[:, 0:16, :], b_rows, over, preferred_element_type=F32)
    last = lax.dot_general(message[:, 16:32, :], b_rows, over, preferred_element_type=F32)
    edges = message[:, 48:64, :].astype(F32)
    kept_inner_ref[:, :, 0:128] = edges[:, 0:3, :].astype(BF16)
    kept_inner_ref[:, :, 128:192] = edges[:, 3:6, 0:64].astype(BF16)
    kept_shared_ref[:, :, 0:128] = edges[:, 6:9, :].astype(BF16)
    kept_shared_ref[:, :, 128:256] = edges[:, 9:12, :].astype(BF16)
    decay = edges[:, 12:13, :] + edges[:, 13:14, :]
    for head in range(3):
        low = 64 * head
        added = first[:, low : low + 64, :] if head < 2 else last[:, 0:64, :]
        kept_ref[:, low : low + 64, :] = (
            state_out[:, low : low + 64, :].astype(F32) * decay[:, :, head : head + 1] + added
        ).astype(BF16)


def whole(memory_space=pltpu.VMEM):
    return pl.BlockSpec(memory_space=memory_space)


def local(
    count,
    hidden,
    start_state,
    tail_inner,
    tail_shared,
    input_gain,
    w_gate_inner,
    w_shared,
    w_step,
    step_bias,
    decay_log,
    conv_inner,
    conv_inner_bias,
    conv_shared,
    conv_shared_bias,
    skip_gain,
    gated_gain,
    w_output,
    next_gain,
    w_next,
    dealing,
    accepted,
    owners,
):
    tokens, block = hidden.shape
    requests, heads, head_size, states = start_state.shape
    length = tokens // requests
    start = start_state.reshape(requests, heads * head_size, states)
    table, accepted_rows = pl.pallas_call(
        table_kernel,
        out_shape=(
            jax.ShapeDtypeStruct((8, 128), jnp.int32),
            jax.ShapeDtypeStruct((tokens, 1), jnp.int32),
        ),
        in_specs=[whole()] * 3,
        out_specs=(whole(), whole()),
        scratch_shapes=[pltpu.VMEM((dealing.shape[0], 8), F32)],
    )(dealing[None, :], owners[None, :], accepted[None, :])

    def pad_tail(tail):
        kept_rows = tail.shape[1]
        return jnp.pad(tail, ((0, 0), (length - kept_rows, 0), (0, 0))).reshape(
            tokens, tail.shape[2]
        )

    def lanes(row):
        return jnp.pad(row, (0, 128 - row.shape[0]))[None, :]

    w_gate = w_gate_inner[:, :block].reshape(count, block, block)
    w_inner = w_gate_inner[:, block:].reshape(count, block, block)
    w_small = jnp.concatenate(
        [
            w_step,
            jnp.zeros((w_step.shape[0], 32 - heads), BF16),
            w_shared,
            jnp.zeros((w_step.shape[0], 64), BF16),
        ],
        axis=1,
    ).reshape(count, block, 128)
    w_out = w_output.reshape(block, count, block).transpose(1, 0, 2)
    routed = []
    for rows in (heads * head_size // 2, 32):
        routed += [
            pltpu.VMEM((2, 112, rows, 128), BF16),
            pltpu.VMEM((2, 2, 16, rows, 128), BF16),
            pltpu.VMEM((2, 2, 32, rows, 128), BF16),
            pltpu.VMEM((2, 32, rows, 128), BF16),
            pltpu.VMEM((2, 2, 48, rows, 128), BF16),
        ]
    new_part, next_input, kept, kept_inner, kept_shared = pl.pallas_call(
        functools.partial(layer_kernel, count, SIDE),
        out_shape=(
            jax.ShapeDtypeStruct((tokens, block), BF16),
            jax.ShapeDtypeStruct((tokens, w_next.shape[1]), BF16),
            jax.ShapeDtypeStruct(start.shape, BF16),
            jax.ShapeDtypeStruct(tail_inner.shape, BF16),
            jax.ShapeDtypeStruct(tail_shared.shape, BF16),
        ),
        in_specs=[whole(pltpu.SMEM)] + [whole()] * 20,
        out_specs=(whole(),) * 5,
        scratch_shapes=[
            pltpu.VMEM((count, tokens, block), BF16),
            pltpu.VMEM((tokens, 128), BF16),
            pltpu.VMEM((count, tokens, 128), BF16),
            pltpu.VMEM((8, tokens), F32),
            pltpu.VMEM((count, 8, tokens), F32),
            pltpu.VMEM((count, tokens, block), BF16),
            pltpu.VMEM((count, tokens, block), BF16),
            pltpu.VMEM((count, tokens, block), BF16),
            pltpu.VMEM((requests, 64, 128), BF16),
            pltpu.VMEM(start.shape, BF16),
            *routed,
            pltpu.SemaphoreType.DMA((5,)),
            pltpu.SemaphoreType.DMA((5,)),
            pltpu.SemaphoreType.DMA((64,)),
            pltpu.SemaphoreType.DMA((64,)),
        ],
        compiler_params=pltpu.CompilerParams(
            collective_id=0, has_side_effects=True, vmem_limit_bytes=58 << 20
        ),
        cost_estimate=pl.CostEstimate(
            flops=4_000_000_000, bytes_accessed=100_000_000, transcendentals=0
        ),
    )(
        table,
        accepted_rows,
        hidden,
        start,
        pad_tail(tail_inner),
        pad_tail(tail_shared),
        input_gain.reshape(count, 1, block),
        w_gate,
        w_inner,
        w_small,
        lanes(step_bias),
        lanes(decay_log),
        conv_inner,
        conv_inner_bias[None, :],
        conv_shared,
        conv_shared_bias[None, :],
        jnp.repeat(skip_gain, head_size)[None, :],
        gated_gain[None, :],
        w_out,
        next_gain.reshape(count, 1, block),
        w_next.reshape(count, block, w_next.shape[1]),
    )
    return (new_part, next_input, kept.reshape(start_state.shape), kept_inner, kept_shared)


def solution(mesh):
    placed = (
        P("wide", "narrow"),
        P("wide", "narrow", None, None),
        P("wide", None, "narrow"),
        P("wide", None, None),
        P(),
        P(None, "narrow"),
        P(None, "narrow"),
        P(None, "narrow"),
        P("narrow"),
        P("narrow"),
        P(None, "narrow"),
        P("narrow"),
        P(),
        P(),
        P("narrow"),
        P("narrow"),
        P("narrow", None),
        P(),
        P(None, "narrow"),
        P(),
        P(),
        P(),
    )
    return jax.shard_map(
        functools.partial(local, mesh.shape["narrow"]),
        mesh=mesh,
        in_specs=placed,
        out_specs=(
            P("wide", "narrow"),
            P("wide", "narrow"),
            P("wide", "narrow", None, None),
            P("wide", None, "narrow"),
            P("wide", None, None),
        ),
        check_vma=False,
    )
```

time: 220 us -> 142 us (0.65)
  Pallas kernels: 0 us -> 117 us
  waiting for transfers between devices: 49.5 us -> 0 us
  blocking collectives: 46.4 us -> 0 us
  starting transfers between devices: 33 us -> 0 us
  other arithmetic: 30.4 us -> 1.02 us
  matrix products: 22.6 us -> 0 us
  between operations: 14.6 us -> 0.71 us
    pallas_call x0 -> x2, Pallas kernels: none -> 117 us  [the longest x1 109 us: local(): pl.pallas_call(functools.partial(layer_kernel, count, SIDE), out_shape=(j...]
    psum x1 -> x0, waiting for transfers between devices: 46.1 us -> none  [local(): lax.psum(partial_sum.astype(jnp.bfloat16), 'narrow').astype(jnp.float32)]
    all_gather x2 -> x0, blocking collectives: 33.2 us -> none  [the longest x1 20.2 us: local(): full_rows = lax.all_gather(hidden, 'narrow', axis=1, tiled=True)]
    all_to_all x3 -> x0, starting transfers between devices: 32.9 us -> none  [the longest x1 12.4 us: local(): lax.all_to_all(shared_bucket, 'wide', split_axis=0, concat_axis=0, tiled=...]
    dot_general x18 -> x0, matrix products: 22.6 us -> none  [the longest x1 3.81 us: state_block(): jnp.einsum('rsh,rshp,rsn->rhpn', factor, inner, b_part, precision=HIGHEST)]
    another operation x4 -> x0, other arithmetic: 18.8 us -> none
    psum x1 -> x0, blocking collectives: 13.2 us -> none  [local(): squares = lax.psum(jnp.sum(gated * gated, axis=1, keepdims=True), 'narrow')]
    gather x3 -> x0, local copies, waits for them, and re-layouts: 10.4 us -> none  [the longest x1 4.53 us: local(): slot_owner = jnp.take(owners, dealing)]
  transfers between devices with their start and end apart: 4 -> 0, of which waited for: 2 -> 0; matrix products, arithmetic and copies ran while one was open for 26% -> 0% of each run, Pallas kernels for 0% -> 0%
where the time goes in v1:
time: 142 us
  Pallas kernels  117 us (82%)
  local copies, waits for them, and re-layouts  23.3 us (16%)
    pallas_call x1, Pallas kernels, local(): pl.pallas_call(functools.partial(layer_kernel, count, SIDE), out_shape=(j...  109 us
    unnamed x21, local copies, waits for them, and re-layouts  13.2 us
    pallas_call x1, Pallas kernels, local(): pl.pallas_call(table_kernel, out_shape=(jax.ShapeDtypeStruct((8, 128), jn...  8 us

profile of v1, /device:TPU:1, one launch (start us, length us, event | category | flops | bytes accessed | tf_op | source)
XLA Modules:
  0.0 141.7 jit_solution(3327875084222239639)
XLA Ops:
  0.6 0.0 copy-start.4
  0.7 0.1 pad.22.clone
  0.7 0.1 pad.20.clone
  0.8 1.3 pad_bitcast_fusion
  2.1 0.7 broadcast_in_dim.42
  2.8 0.6 broadcast_in_dim_reshape.3.skip_ref
  3.5 1.4 reshape.46.gain_ref
  4.8 1.4 reshape.51.next_gain_ref
  6.2 0.8 copy.48
  7.0 0.8 copy.49
  7.7 0.7 pad.16.clone
  8.4 0.0 copy-start.3
  8.4 0.7 pad.15.clone
  9.1 1.7 %copy.43.hidden_ref = bf16[256,192]{1,0:T(8,128)(2,1)} copy(bf16[256,192]{0,1:T(8,128)(2,1)} %param.22) | data formatting | bytes 196608 | tf_op args[0]
  10.7 8.0 %shard_map.245 = (s32[8,128]{1,0:T(8,128)}, s32[256,1]{1,0:T(8,128)}) custom-call(s32[1,1024]{1,0:T(1,128)} %bitcast.29, s32[1,1024]{1,0:T(1,128)} %bitcast.30, s32[1,1024]{1,0:T(1,128)} %bitcast.31), custom_call_target="tpu_custom_call" | custom-call | tf_op jit(solution)/shard_map/pallas_call | solution.py:638
  18.7 1.1 copy.40
  19.9 0.0 copy-done.4
  19.9 0.3 copy.39
  20.1 1.0 maximum_maximum_fusion
  21.2 0.0 copy-done.3
  21.2 0.0 copy-start.1
  21.2 0.6 reshape.50
  21.8 1.0 copy.51
  22.8 0.0 copy-done.1
  22.8 0.0 copy-start
  22.8 1.6 %copy.42 = bf16[1536,403]{1,0:T(8,128)(2,1)} copy(bf16[1536,403]{0,1:T(8,128)(2,1)S(1)} %copy-done.1) | data formatting | bytes 2476032 | tf_op args[18]
  24.4 0.0 copy-done
  24.4 1.5 %fusion = (bf16[1536,192]{1,0:T(8,128)(2,1)}, bf16[1536,192]{1,0:T(8,128)(2,1)}) fusion(bf16[1536,384]{1,0:T(8,128)(2,1)S(1)} %copy-done), kind=kLoop, calls=%fused_computation.4 | loop fusion | bytes 2359296 | tf_op jit(solution)/shard_map/slice | solution.py:659
  25.9 108.8 %shard_map.246 = (bf16[256,192]{1,0:T(8,128)(2,1)}, bf16[256,403]{1,0:T(8,128)(2,1)}, bf16[16,192,128]{2,1,0:T(8,128)(2,1)}, bf16[16,3,192]{2,1,0:T(4,128)(2,1)}, bf16[16,3,256]{2,1,0:T(4,128)(2,1)}) custom-call(s32[8,128]{1,0:T(8,128)} %get-tuple-element.12.table_ref, s32[256,1]{1,0:T(8,128)} %get-tuple-element.13.acc_ref, ...), custom_call_target="tpu_custom_call" | custom-call | flops 4000000000 | bytes 100000000 | tf_op jit(solution)/shard_map/pallas_call | solution.py:679
  134.6 0.0 copy-start.2
  134.6 1.7 %copy.44 = bf16[256,192]{0,1:T(8,128)(2,1)} copy(bf16[256,192]{1,0:T(8,128)(2,1)} %get-tuple-element.24) | data formatting | bytes 196608
  136.4 1.4 copy.46
  137.7 1.4 copy.47
  139.1 1.8 %copy.45 = bf16[256,403]{0,1:T(8,128)(2,1)} copy(bf16[256,403]{1,0:T(8,128)(2,1)} %get-tuple-element.25) | data formatting | bytes 412672
  140.9 0.0 copy-done.2
  140.9 0.9 copy.53
  (2 shorter events, 0.0 us)
Async XLA Ops:
  0.6 19.2 %copy-start.4 = (bf16[1536,3]{0,1:T(4,128)(2,1)S(1)}, bf16[1536,3]{0,1:T(4,128)(2,1)}, u32[]{:S(2)}) copy-start(bf16[1536,3]{0,1:T(4,128)(2,1)} %param.29) | copy-start | bytes 27652
  8.4 12.8 %copy-start.3 = (bf16[192,1536]{1,0:T(8,128)(2,1)S(1)}, bf16[192,1536]{1,0:T(8,128)(2,1)}, u32[]{:S(2)}) copy-start(bf16[192,1536]{1,0:T(8,128)(2,1)} %param.38) | copy-start | bytes 1769476
  21.2 1.6 %copy-start.1 = (bf16[1536,403]{0,1:T(8,128)(2,1)S(1)}, bf16[1536,403]{0,1:T(8,128)(2,1)}, u32[]{:S(2)}) copy-start(bf16[1536,403]{0,1:T(8,128)(2,1)} %param.40) | copy-start | bytes 3714052
  22.8 1.6 %copy-start = (bf16[1536,384]{1,0:T(8,128)(2,1)S(1)}, bf16[1536,384]{1,0:T(8,128)(2,1)}, u32[]{:S(2)}) copy-start(bf16[1536,384]{1,0:T(8,128)(2,1)} %param.27) | copy-start | bytes 3538948
  134.6 6.2 %copy-start.2 = (bf16[16,192,128]{2,1,0:T(8,128)(2,1)S(1)}, bf16[16,192,128]{2,1,0:T(8,128)(2,1)}, u32[]{:S(2)}) copy-start(bf16[16,192,128]{2,1,0:T(8,128)(2,1)} %get-tuple-element.16) | copy-start | bytes 2359300

commit v2 on v1

--- a/solution.py
+++ b/solution.py
@@ -80,7 +80,9 @@
     for h in (0, 1):
         back1, dist1, back2, dist2 = halves[h]
         pos1, pos2 = places[2 * h], places[2 * h + 1]
-        loc = jnp.where(dist1 == 0, ln & 15, 16 + back1 * 48 + hop_base(dist1) + pos1)
+        loc = jnp.where(
+            dist1 == 0, ln & 15, jnp.minimum(16 + back1 * 48 + hop_base(dist1) + pos1, 111)
+        )
         out.append(lookup(me * 32 + t, sender * 32 + back1 * 16 + pos1, ln & 15, 0))
         back_t = jnp.where(t >= 48, 1, 0)
         q = t - 48 * back_t
@@ -92,7 +94,7 @@
         else:
             dest = me_y * SIDE + ((me_z + move) & 7)
         out.append(lookup(((dest * 2 + back_t) * 8 + hop) * 16 + i, ((owner * 2 + back2) * 8 + dist2) * 16 + pos2, loc, -1))
-        out.append(lookup(me * 16 + t, owner * 16 + places[4], jnp.where(dist2 == 0, loc, 128 + back2 * 16 + pos2), 0))
+        out.append(lookup(me * 16 + t, owner * 16 + places[4], jnp.where(dist2 == 0, loc, 128 + jnp.minimum(back2 * 16 + pos2, 31)), 0))
     out.append(lookup(me * 16 + t, ln, acc, 0))
     out.append(out[-1])
     r = lax.broadcasted_iota(jnp.int32, (8, 128), 0)
@@ -144,9 +146,8 @@
 
 class Route:
     def __init__(self, number, table, refs, send_sem, recv_sem, side):
-        self.number, self.table, self.send_sem, self.recv_sem, self.side = (
-            number, table, send_sem, recv_sem, side
-        )
+        self.number, self.table = number, table
+        self.send_sem, self.recv_sem, self.side = send_sem, recv_sem, side
         self.pool, self.lists, self.passing, self.final, self.second = refs
 
     def neighbour(self, half, back, phase):
@@ -198,7 +199,7 @@
             for back in (0, 1):
 
                 def listed(i, carry):
-                    self.lists[half, back, i] = blocks[self.table[3 * half, 16 * back + i], low : low + rows, :]
+                    self.lists[half, back, i] = blocks[jnp.clip(self.table[3 * half, 16 * back + i], 0, 15), low : low + rows, :]
                     return carry
 
                 lax.fori_loop(0, 16, listed, 0)
@@ -225,14 +226,14 @@
 
                 def merged(i, carry):
                     at = self.table[3 * half + 1, 48 * back + low + i]
-                    mine = self.pool[half, jnp.maximum(at, 0)]
+                    mine = self.pool[half, jnp.clip(at, 0, 111)]
                     came = self.passing[half, back, SECOND_OFFS[hop - 1] + i]
                     self.second[half, back, low + i] = jnp.where(at >= 0, mine, came)
                     return carry
 
                 def fresh(i, carry):
                     at = self.table[3 * half + 1, 48 * back + low + i]
-                    self.second[half, back, low + i] = self.pool[half, jnp.maximum(at, 0)]
+                    self.second[half, back, low + i] = self.pool[half, jnp.clip(at, 0, 111)]
                     return carry
 
                 if known:
@@ -248,8 +249,8 @@
 
             def take(k, carry):
                 at = self.table[3 * half + 2, k]
-                here = self.pool[half, jnp.where(at < 128, at, 0)]
-                came = self.final[half, jnp.where(at < 128, 0, at - 128)]
+                here = self.pool[half, jnp.clip(jnp.where(at < 128, at, 0), 0, 111)]
+                came = self.final[half, jnp.clip(at - 128, 0, 31)]
                 blocks[k, low : low + rows, :] = jnp.where(at < 128, here, came)
                 return carry
 
@@ -266,22 +267,22 @@
     count,
     side,
     table_ref,
+    bias_ref,
+    decay_ref,
+    skip_ref,
     acc_ref,
     hidden_ref,
     start_ref,
     tail_inner_ref,
     tail_shared_ref,
     gain_ref,
-    w_gate_ref,
-    w_inner_ref,
-    w_small_ref,
-    bias_ref,
-    decay_ref,
+    w_gate_inner_ref,
+    w_shared_ref,
+    w_step_ref,
     conv_inner_ref,
     conv_inner_bias_ref,
     conv_shared_ref,
     conv_shared_bias_ref,
-    skip_ref,
     gated_gain_ref,
     w_out_ref,
     next_gain_ref,
@@ -299,6 +300,7 @@
     part_out,
     part_buf,
     new_buf,
+    stack,
     message,
     state_out,
     state_pool,
@@ -333,7 +335,7 @@
         route_recv,
         side,
     )
-    tokens, block = hidden_ref.shape
+    block, tokens = hidden_ref.shape
     requests = start_ref.shape[0]
     length = tokens // requests
     width = block * count
@@ -390,44 +392,55 @@
     place = rows[:, :1] & (length - 1)
     acc = acc_ref[...]
     lane = lax.broadcasted_iota(jnp.int32, (tokens, block), 1)
+    small_eye = lax.broadcasted_iota(jnp.int32, (block, block), 0) == lax.broadcasted_iota(
+        jnp.int32, (block, block), 1
+    )
+    turn = small_eye.astype(BF16)
 
     def to_row(column):
         return jnp.sum(jnp.where(eye, column, 0.0), axis=0, keepdims=True)
 
-    def to_column(row):
-        return jnp.sum(jnp.where(eye, row, 0.0), axis=1, keepdims=True)
+    def gain_column(gains, n):
+        return jnp.sum(
+            jnp.where(small_eye, gains[:, n * block : (n + 1) * block], 0.0), axis=1, keepdims=True
+        )
 
     def spread(values):
         return jnp.where(
             lane < 64, values[:, 0:1], jnp.where(lane < 128, values[:, 1:2], values[:, 2:3])
         )
 
+    def scalars(ref, where, limit):
+        return jnp.where(where < limit, ref[0], jnp.where(where < 2 * limit, ref[1], ref[2]))
+
     def normed(buf, gains):
-        total = jnp.zeros((tokens, 1), F32)
+        total = jnp.zeros((1, tokens), F32)
         for n in range(count):
             piece = buf[n].astype(F32)
-            total = total + jnp.sum(piece * piece, axis=1, keepdims=True)
+            total = total + jnp.sum(piece * piece, axis=0, keepdims=True)
         factor = lax.rsqrt(total / width + EPSILON)
-        return [(buf[n].astype(F32) * factor * gains[n]).astype(BF16) for n in range(count)]
-
+        for n in range(count):
+            stack[n * block : (n + 1) * block, :] = (
+                buf[n].astype(F32) * factor * gains[n]
+            ).astype(BF16)
+
+    gains_now = gain_ref[...].reshape(1, width)
+    gains_now = [gain_column(gains_now, n) for n in range(count)]
     states.first(1)
     finish(gather_buf, 0)
-    gate = jnp.zeros((tokens, block), F32)
-    inner = jnp.zeros((tokens, block), F32)
-    small = jnp.zeros((tokens, 128), F32)
-    pieces = normed(gather_buf, gain_ref)
-    for n in range(count):
-        small = small + bdot(pieces[n], w_small_ref[n])
-    small_out[...] = small.astype(BF16)
+    normed(gather_buf, gains_now)
+    upright = (((0,), (0,)), ((), ()))
+    small_out[...] = bdot(w_shared_ref[...], stack[...]).astype(BF16)
     for step in range(1, count):
         send(small_out, small_buf, 1, step)
     small_buf[me] = small_out[...]
-    for n in range(count):
-        inner = inner + bdot(pieces[n], w_inner_ref[n])
-        gate = gate + bdot(pieces[n], w_gate_ref[n])
-    gate = gate.astype(BF16).astype(F32)
+    step_raw = bdot(w_step_ref[...], stack[...]).astype(BF16)
+    both = lax.dot_general(
+        w_gate_inner_ref[...], stack[...], upright, preferred_element_type=F32
+    ).astype(BF16)
+    gate = lax.dot_general(both[:block], turn, upright, preferred_element_type=F32)
+    inner_bf = lax.dot_general(both[block:], turn, upright, preferred_element_type=F32).astype(BF16)
     states.first(2)
-    inner_bf = inner.astype(BF16)
 
     def filtered(fresh, tail, weight, offset):
         total = offset + fresh * weight[3:4]
@@ -440,8 +453,18 @@
             total = total + moved * weight[3 - shift : 4 - shift]
         return jax.nn.silu(total)
 
-    tail_inner = tail_inner_ref[...]
-    tail_shared = tail_shared_ref[...]
+    def padded(ref):
+        total = jnp.zeros((tokens, ref.shape[2]), F32)
+        at = lax.broadcasted_iota(jnp.int32, (tokens, requests), 0)
+        slot = lax.broadcasted_iota(jnp.int32, (tokens, requests), 1)
+        kept_rows = ref.shape[0]
+        for q in range(kept_rows):
+            put = ((at >> 4) == slot) & ((at & (length - 1)) == length - kept_rows + q)
+            total = total + bdot(put.astype(BF16), ref[q])
+        return total.astype(BF16)
+
+    tail_inner = padded(tail_inner_ref)
+    tail_shared = padded(tail_shared_ref)
     conv_i = filtered(
         inner_bf.astype(F32),
         tail_inner.astype(F32),
@@ -449,9 +472,15 @@
         conv_inner_bias_ref[...],
     )
 
-    raw = small.astype(BF16).astype(F32) + bias_ref[...]
+    heads = w_step_ref.shape[0]
+    head_lane = lax.broadcasted_iota(jnp.int32, (heads, 128), 1)
+    head_eye = (head_lane == lax.broadcasted_iota(jnp.int32, (heads, 128), 0)).astype(BF16)
+    lane_row = lax.broadcasted_iota(jnp.int32, (1, 128), 1)
+    raw = lax.dot_general(step_raw, head_eye, upright, preferred_element_type=F32) + scalars(
+        bias_ref, lane_row, 1
+    )
     steps = jnp.maximum(raw, 0.0) + jnp.log1p(jnp.exp(-jnp.abs(raw)))
-    log_decay = steps * -jnp.exp(decay_ref[...])
+    log_decay = steps * -jnp.exp(scalars(decay_ref, lane_row, 1))
     cumul = fdot(tri.astype(F32), log_decay)
     col_place = cols & (length - 1)
     ending = fdot((same & (col_place < acc)).astype(F32), log_decay)
@@ -462,12 +491,12 @@
 
     states.first(3)
     finish(small_buf, 1)
-    lane_in = lax.broadcasted_iota(jnp.int32, (128, 256), 0)
-    lane_out = lax.broadcasted_iota(jnp.int32, (128, 256), 1)
-    shared = jnp.zeros((tokens, 256), F32)
-    for n in range(count):
-        pick = (lane_in >= 32) & (lane_in < 64) & (lane_out == lane_in - 32 + 32 * n)
-        shared = shared + bdot(small_buf[n], pick.astype(BF16))
+    shared = lax.dot_general(
+        small_buf[...].reshape(tokens, tokens),
+        eye.astype(BF16),
+        upright,
+        preferred_element_type=F32,
+    )
     conv_s = filtered(
         shared, tail_shared.astype(F32), conv_shared_ref[...].astype(F32), conv_shared_bias_ref[...]
     )
@@ -531,7 +560,7 @@
         precision=HIGHEST,
         preferred_element_type=F32,
     ).reshape(tokens, block)
-    outputs = carried * spread(jnp.exp(cumul)) + direct + skip_ref[...] * conv_i
+    outputs = carried * spread(jnp.exp(cumul)) + direct + scalars(skip_ref, lane, 64) * conv_i
     gated = outputs * jax.nn.silu(gate)
     square_out[...] = lax.dot_general(
         jnp.ones((8, block), F32),
@@ -544,11 +573,17 @@
         send(square_out, square_buf, 2, step)
     square_buf[me] = square_out[...]
     scaled = (gated * gated_gain_ref[...]).astype(BF16)
+    scaled = lax.dot_general(
+        turn, scaled, (((1,), (1,)), ((), ())), preferred_element_type=F32
+    ).astype(BF16)
+    part_out[...] = (
+        lax.dot_general(w_out_ref[...], scaled, upright, preferred_element_type=F32)
+        .astype(BF16)
+        .reshape(count, block, tokens)
+    )
     for step in range(1, count):
-        towards = lax.rem(me + step, count)
-        part_out[towards] = bdot(scaled, w_out_ref[towards]).astype(BF16)
-        send(part_out.at[towards], part_buf, 3, step)
-    part_buf[me] = bdot(scaled, w_out_ref[me]).astype(BF16)
+        send(part_out.at[lax.rem(me + step, count)], part_buf, 3, step)
+    part_buf[me] = part_out[me]
 
     updates.first(2)
     states.after(2)
@@ -556,7 +591,7 @@
     squares = square_buf[0]
     for n in range(1, count):
         squares = squares + square_buf[n]
-    factor_out = lax.rsqrt(to_column(squares[0:1]) / width + EPSILON)
+    factor_out = lax.rsqrt(squares[0:1] / width + EPSILON)
     finish(part_buf, 3)
     summed = part_buf[0].astype(F32)
     for n in range(1, count):
@@ -568,11 +603,9 @@
     updates.first(3)
     states.after(3)
     finish(new_buf, 4)
-    pieces = normed(new_buf, next_gain_ref)
-    projected = jnp.zeros(next_ref.shape, F32)
-    for n in range(count):
-        projected = projected + bdot(pieces[n], w_next_ref[n])
-    next_ref[...] = projected.astype(BF16)
+    gains_next = next_gain_ref[...].reshape(1, width)
+    normed(new_buf, [gain_column(gains_next, n) for n in range(count)])
+    next_ref[...] = bdot(w_next_ref[...], stack[...]).astype(BF16)
     updates.first(4)
     updates.after(0)
     updates.after(1)
@@ -589,10 +622,13 @@
     first = lax.dot_general(message[:, 0:16, :], b_rows, over, preferred_element_type=F32)
     last = lax.dot_general(message[:, 16:32, :], b_rows, over, preferred_element_type=F32)
     edges = message[:, 48:64, :].astype(F32)
-    kept_inner_ref[:, :, 0:128] = edges[:, 0:3, :].astype(BF16)
-    kept_inner_ref[:, :, 128:192] = edges[:, 3:6, 0:64].astype(BF16)
-    kept_shared_ref[:, :, 0:128] = edges[:, 6:9, :].astype(BF16)
-    kept_shared_ref[:, :, 128:256] = edges[:, 9:12, :].astype(BF16)
+    swap = ((rows >> 4) == (cols & 15)) & ((rows & 15) == (cols >> 4))
+    by_row = bdot(swap.astype(BF16), message[:, 48:64, :].reshape(tokens, 128)).astype(BF16)
+    for q in range(3):
+        kept_inner_ref[q, :, 0:128] = by_row[16 * q : 16 * q + 16]
+        kept_inner_ref[q, :, 128:192] = by_row[48 + 16 * q : 64 + 16 * q, 0:64]
+        kept_shared_ref[q, :, 0:128] = by_row[96 + 16 * q : 112 + 16 * q]
+        kept_shared_ref[q, :, 128:256] = by_row[144 + 16 * q : 160 + 16 * q]
     decay = edges[:, 12:13, :] + edges[:, 13:14, :]
     for head in range(3):
         low = 64 * head
@@ -633,8 +669,17 @@
 ):
     tokens, block = hidden.shape
     requests, heads, head_size, states = start_state.shape
-    length = tokens // requests
     start = start_state.reshape(requests, heads * head_size, states)
+    routed = []
+    for rows in (heads * head_size // 2, 32):
+        routed += [
+            pltpu.VMEM((2, 112, rows, 128), BF16),
+            pltpu.VMEM((2, 2, 16, rows, 128), BF16),
+            pltpu.VMEM((2, 2, 32, rows, 128), BF16),
+            pltpu.VMEM((2, 32, rows, 128), BF16),
+            pltpu.VMEM((2, 2, 48, rows, 128), BF16),
+        ]
+    shared_here = w_shared.shape[1]
     table, accepted_rows = pl.pallas_call(
         table_kernel,
         out_shape=(
@@ -645,57 +690,51 @@
         out_specs=(whole(), whole()),
         scratch_shapes=[pltpu.VMEM((dealing.shape[0], 8), F32)],
     )(dealing[None, :], owners[None, :], accepted[None, :])
-
-    def pad_tail(tail):
-        kept_rows = tail.shape[1]
-        return jnp.pad(tail, ((0, 0), (length - kept_rows, 0), (0, 0))).reshape(
-            tokens, tail.shape[2]
-        )
-
-    def lanes(row):
-        return jnp.pad(row, (0, 128 - row.shape[0]))[None, :]
-
-    w_gate = w_gate_inner[:, :block].reshape(count, block, block)
-    w_inner = w_gate_inner[:, block:].reshape(count, block, block)
-    w_small = jnp.concatenate(
-        [
-            w_step,
-            jnp.zeros((w_step.shape[0], 32 - heads), BF16),
-            w_shared,
-            jnp.zeros((w_step.shape[0], 64), BF16),
-        ],
-        axis=1,
-    ).reshape(count, block, 128)
-    w_out = w_output.reshape(block, count, block).transpose(1, 0, 2)
-    routed = []
-    for rows in (heads * head_size // 2, 32):
-        routed += [
-            pltpu.VMEM((2, 112, rows, 128), BF16),
-            pltpu.VMEM((2, 2, 16, rows, 128), BF16),
-            pltpu.VMEM((2, 2, 32, rows, 128), BF16),
-            pltpu.VMEM((2, 32, rows, 128), BF16),
-            pltpu.VMEM((2, 2, 48, rows, 128), BF16),
-        ]
+    operands = (
+        table,
+        step_bias,
+        decay_log,
+        skip_gain,
+        accepted_rows,
+        hidden.T,
+        start,
+        tail_inner.transpose(1, 0, 2),
+        tail_shared.transpose(1, 0, 2),
+        input_gain,
+        w_gate_inner,
+        w_shared.T,
+        w_step.T,
+        conv_inner,
+        conv_inner_bias[None, :],
+        conv_shared,
+        conv_shared_bias[None, :],
+        gated_gain[None, :],
+        w_output,
+        next_gain,
+        w_next.T,
+    )
+    blocks = pltpu.VMEM((count, block, tokens), BF16)
     new_part, next_input, kept, kept_inner, kept_shared = pl.pallas_call(
         functools.partial(layer_kernel, count, SIDE),
         out_shape=(
-            jax.ShapeDtypeStruct((tokens, block), BF16),
-            jax.ShapeDtypeStruct((tokens, w_next.shape[1]), BF16),
+            jax.ShapeDtypeStruct((block, tokens), BF16),
+            jax.ShapeDtypeStruct((w_next.shape[1], tokens), BF16),
             jax.ShapeDtypeStruct(start.shape, BF16),
-            jax.ShapeDtypeStruct(tail_inner.shape, BF16),
-            jax.ShapeDtypeStruct(tail_shared.shape, BF16),
+            jax.ShapeDtypeStruct((3, requests, tail_inner.shape[2]), BF16),
+            jax.ShapeDtypeStruct((3, requests, tail_shared.shape[2]), BF16),
         ),
-        in_specs=[whole(pltpu.SMEM)] + [whole()] * 20,
+        in_specs=[whole(pltpu.SMEM)] * 4 + [whole()] * (len(operands) - 4),
         out_specs=(whole(),) * 5,
         scratch_shapes=[
-            pltpu.VMEM((count, tokens, block), BF16),
-            pltpu.VMEM((tokens, 128), BF16),
-            pltpu.VMEM((count, tokens, 128), BF16),
+            blocks,
+            pltpu.VMEM((shared_here, tokens), BF16),
+            pltpu.VMEM((count, shared_here, tokens), BF16),
             pltpu.VMEM((8, tokens), F32),
             pltpu.VMEM((count, 8, tokens), F32),
-            pltpu.VMEM((count, tokens, block), BF16),
-            pltpu.VMEM((count, tokens, block), BF16),
-            pltpu.VMEM((count, tokens, block), BF16),
+            blocks,
+            blocks,
+            blocks,
+            pltpu.VMEM((count * block, tokens), BF16),
             pltpu.VMEM((requests, 64, 128), BF16),
             pltpu.VMEM(start.shape, BF16),
             *routed,
@@ -710,30 +749,14 @@
         cost_estimate=pl.CostEstimate(
             flops=4_000_000_000, bytes_accessed=100_000_000, transcendentals=0
         ),
-    )(
-        table,
-        accepted_rows,
-        hidden,
-        start,
-        pad_tail(tail_inner),
-        pad_tail(tail_shared),
-        input_gain.reshape(count, 1, block),
-        w_gate,
-        w_inner,
-        w_small,
-        lanes(step_bias),
-        lanes(decay_log),
-        conv_inner,
-        conv_inner_bias[None, :],
-        conv_shared,
-        conv_shared_bias[None, :],
-        jnp.repeat(skip_gain, head_size)[None, :],
-        gated_gain[None, :],
-        w_out,
-        next_gain.reshape(count, 1, block),
-        w_next.reshape(count, block, w_next.shape[1]),
-    )
-    return (new_part, next_input, kept.reshape(start_state.shape), kept_inner, kept_shared)
+    )(*operands)
+    return (
+        new_part.T,
+        next_input.T,
+        kept.reshape(start_state.shape),
+        kept_inner.transpose(1, 0, 2),
+        kept_shared.transpose(1, 0, 2),
+    )
 
 
 def solution(mesh):

time: 142 us -> 120 us (0.85); the launches traced: 142 us -> 118 us
  local copies, waits for them, and re-layouts: 23.3 us -> 6.46 us
  Pallas kernels: 117 us -> 111 us
    unnamed x21 -> x9, local copies, waits for them, and re-layouts: 13.2 us -> 6.46 us
    pallas_call x1, Pallas kernels: 109 us -> 103 us  [local(): pl.pallas_call(functools.partial(layer_kernel, count, SIDE), out_shape=(j...]
    reshape x4 -> x0, local copies, waits for them, and re-layouts: 4.38 us -> none  [the longest x2 1.63 us: local(): w_out = w_output.reshape(block, count, block).transpose(1, 0, 2)]
    broadcast_in_dim x4 -> x0, local copies, waits for them, and re-layouts: 2 us -> none  [the longest x1 1.27 us: lanes(): return jnp.pad(row, (0, 128 - row.shape[0]))[None, :]]
    slice x1 -> x0, local copies, waits for them, and re-layouts: 1.48 us -> none  [local(): w_inner = w_gate_inner[:, block:].reshape(count, block, block)]
where the time goes in v2:
time: 120 us; the launch traced here: 118 us
  Pallas kernels  111 us (92%)
  local copies, waits for them, and re-layouts  6.46 us (5%)
    pallas_call x1, Pallas kernels, local(): pl.pallas_call(functools.partial(layer_kernel, count, SIDE), out_shape=(j...  103 us
    pallas_call x1, Pallas kernels, local(): pl.pallas_call(table_kernel, out_shape=(jax.ShapeDtypeStruct((8, 128), jn...  8.01 us
    unnamed x9, local copies, waits for them, and re-layouts  6.46 us

profile of v2, /device:TPU:1, one launch (start us, length us, event | category | flops | bytes accessed | tf_op | source)
XLA Modules:
  0.0 117.9 jit_solution(17271799392502643722)
XLA Ops:
  0.6 8.0 %shard_map.245 = (s32[8,128]{1,0:T(8,128)}, s32[256,1]{1,0:T(8,128)}) custom-call(s32[1,1024]{1,0:T(1,128)} %bitcast.23, s32[1,1024]{1,0:T(1,128)} %bitcast.24, s32[1,1024]{1,0:T(1,128)} %bitcast.25), custom_call_target="tpu_custom_call" | custom-call | tf_op jit(solution)/shard_map/pallas_call | solution.py:683
  8.6 102.8 %shard_map.246 = (bf16[192,256]{1,0:T(8,128)(2,1)}, bf16[403,256]{1,0:T(8,128)(2,1)}, bf16[16,192,128]{2,1,0:T(8,128)(2,1)}, bf16[3,16,192]{2,1,0:T(8,128)(2,1)}, bf16[3,16,256]{2,1,0:T(8,128)(2,1)}) custom-call(s32[8,128]{1,0:T(8,128)} %get-tuple-element.12.table_ref, f32[3]{0:T(128)} %bias_ref.1, f32[3]{0:T(128)} %decay_ref.1, f32[3]{0:T(128)} %skip_ref.1, ...), custom_call_target="tpu_custom_call" | custom-call | flops 4000000000 | bytes 100000000 | tf_op jit(solution)/shard_map/pallas_call | solution.py:717
  111.4 0.0 copy-start.1
  111.4 0.0 copy-start
  111.5 1.6 %copy.32 = bf16[256,192]{0,1:T(8,128)(2,1)} copy(bf16[256,192]{0,1:T(8,128)(2,1)} %bitcast.20) | data formatting | bytes 196608
  113.0 1.6 %copy.33 = bf16[256,403]{0,1:T(8,128)(2,1)} copy(bf16[256,403]{0,1:T(8,128)(2,1)} %bitcast.19) | data formatting | bytes 412672
  114.6 2.1 %copy.34 = bf16[16,3,64,128]{3,2,1,0:T(8,128)(2,1)} copy(bf16[16,3,64,128]{3,2,1,0:T(8,128)(2,1)} %bitcast.18) | data formatting | bytes 1572864
  116.7 0.0 copy-done.1
  116.7 0.6 copy.35
  117.3 0.0 copy-done
  117.3 0.6 copy.36
Async XLA Ops:
  111.4 5.3 %copy-start.1 = (bf16[3,16,192]{2,1,0:T(8,128)(2,1)S(1)}, bf16[3,16,192]{2,1,0:T(8,128)(2,1)}, u32[]{:S(2)}) copy-start(bf16[3,16,192]{2,1,0:T(8,128)(2,1)} %get-tuple-element.17) | copy-start | bytes 55300
  111.4 5.9 %copy-start = (bf16[3,16,256]{2,1,0:T(8,128)(2,1)S(1)}, bf16[3,16,256]{2,1,0:T(8,128)(2,1)}, u32[]{:S(2)}) copy-start(bf16[3,16,256]{2,1,0:T(8,128)(2,1)} %get-tuple-element.18) | copy-start | bytes 73732

commit v3 on v2

--- a/solution.py
+++ b/solution.py
@@ -502,6 +502,8 @@
     )
     b_part = conv_s[:, :128]
     c_part = conv_s[:, 128:]
+    states.first(4)
+    states.after(0)
 
     edge = rows[:, :1] & 15
     wanted = jnp.where(
@@ -539,8 +541,7 @@
 
     updates.fill(message, 32)
     updates.first(0)
-    states.first(4)
-    states.after(0)
+    states.after(1)
 
     crossing = lax.dot_general(
         c_part, b_part, (((1,), (1,)), ((), ())), precision=HIGHEST, preferred_element_type=F32
@@ -552,7 +553,6 @@
         mixing = jnp.where(tri, jnp.exp(gap), 0.0) * to_row(steps[:, head : head + 1]) * crossing
         direct = direct + fdot(mixing, jnp.where((lane >> 6) == head, conv_i, 0.0))
     updates.first(1)
-    states.after(1)
     carried = lax.dot_general(
         c_part.reshape(requests, length, 128),
         start_ref[...].astype(F32),
@@ -587,6 +587,9 @@
 
     updates.first(2)
     states.after(2)
+    updates.first(3)
+    updates.first(4)
+    updates.after(0)
     finish(square_buf, 2)
     squares = square_buf[0]
     for n in range(1, count):
@@ -600,21 +603,12 @@
     for step in range(1, count):
         send(new_ref, new_buf, 4, step)
     new_buf[me] = new_ref[...]
-    updates.first(3)
+    updates.after(1)
     states.after(3)
-    finish(new_buf, 4)
-    gains_next = next_gain_ref[...].reshape(1, width)
-    normed(new_buf, [gain_column(gains_next, n) for n in range(count)])
-    next_ref[...] = bdot(w_next_ref[...], stack[...]).astype(BF16)
-    updates.first(4)
-    updates.after(0)
-    updates.after(1)
     updates.after(2)
     updates.after(3)
     states.after(4)
     updates.after(4)
-    states.drain()
-    updates.drain()
     states.collect(state_out, half_rows)
     updates.collect(message, 32)
     over = (((1,), (1,)), ((0,), (0,)))
@@ -636,6 +630,18 @@
         kept_ref[:, low : low + 64, :] = (
             state_out[:, low : low + 64, :].astype(F32) * decay[:, :, head : head + 1] + added
         ).astype(BF16)
+    finish(new_buf, 4)
+    gains_next = next_gain_ref[...].reshape(1, width)
+    normed(new_buf, [gain_column(gains_next, n) for n in range(count)])
+    next_ref[...] = bdot(w_next_ref[...], stack[...]).astype(BF16)
+    states.drain()
+    updates.drain()
+
+
+def hand_over_kernel(*refs):
+    half = len(refs) // 2
+    for source, target in zip(refs[:half], refs[half:]):
+        target[...] = source[...]
 
 
 def whole(memory_space=pltpu.VMEM):
@@ -714,7 +720,7 @@
         w_next.T,
     )
     blocks = pltpu.VMEM((count, block, tokens), BF16)
-    new_part, next_input, kept, kept_inner, kept_shared = pl.pallas_call(
+    results = pl.pallas_call(
         functools.partial(layer_kernel, count, SIDE),
         out_shape=(
             jax.ShapeDtypeStruct((block, tokens), BF16),
@@ -750,6 +756,12 @@
             flops=4_000_000_000, bytes_accessed=100_000_000, transcendentals=0
         ),
     )(*operands)
+    new_part, next_input, kept, kept_inner, kept_shared = pl.pallas_call(
+        hand_over_kernel,
+        out_shape=tuple(jax.ShapeDtypeStruct(one.shape, one.dtype) for one in results),
+        in_specs=[whole()] * 5,
+        out_specs=(whole(),) * 5,
+    )(*results)
     return (
         new_part.T,
         next_input.T,

time: 120 us -> 117 us (0.975)
  the two profiles are of different devices: /device:TPU:1 before, /device:TPU:28 now
where the time goes in v3:
time: 117 us; the launch traced here: 116 us
  Pallas kernels  116 us (99%)
    pallas_call x1, Pallas kernels, local(): pl.pallas_call(functools.partial(layer_kernel, count, SIDE), out_shape=(j...  105 us
    pallas_call x1, Pallas kernels, local(): pl.pallas_call(table_kernel, out_shape=(jax.ShapeDtypeStruct((8, 128), jn...  8.01 us

profile of v3, /device:TPU:28, one launch (start us, length us, event | category | flops | bytes accessed | tf_op | source)
XLA Modules:
  0.0 116.4 jit_solution(6733856252290780529)
XLA Ops:
  0.6 8.0 %shard_map.245 = (s32[8,128]{1,0:T(8,128)}, s32[256,1]{1,0:T(8,128)}) custom-call(s32[1,1024]{1,0:T(1,128)} %bitcast.18, s32[1,1024]{1,0:T(1,128)} %bitcast.19, s32[1,1024]{1,0:T(1,128)} %bitcast.20), custom_call_target="tpu_custom_call" | custom-call | tf_op jit(solution)/shard_map/pallas_call | solution.py:689
  8.6 105.4 %shard_map.246 = (bf16[192,256]{1,0:T(8,128)(2,1)}, bf16[403,256]{1,0:T(8,128)(2,1)}, bf16[16,192,128]{2,1,0:T(8,128)(2,1)}, bf16[3,16,192]{2,1,0:T(8,128)(2,1)}, bf16[3,16,256]{2,1,0:T(8,128)(2,1)}) custom-call(s32[8,128]{1,0:T(8,128)} %get-tuple-element.17.table_ref, f32[3]{0:T(128)} %bias_ref.1, f32[3]{0:T(128)} %decay_ref.1, f32[3]{0:T(128)} %skip_ref.1, ...), custom_call_target="tpu_custom_call" | custom-call | flops 4000000000 | bytes 100000000 | tf_op jit(solution)/shard_map/pallas_call | solution.py:723
  114.1 2.3 %shard_map.247 = (bf16[192,256]{1,0:T(8,128)(2,1)}, bf16[403,256]{1,0:T(8,128)(2,1)}, bf16[16,192,128]{2,1,0:T(8,128)(2,1)}, bf16[3,16,192]{2,1,0:T(8,128)(2,1)}, bf16[3,16,256]{2,1,0:T(8,128)(2,1)}) custom-call(bf16[192,256]{1,0:T(8,128)(2,1)} %get-tuple-element.19.refs_0_, bf16[403,256]{1,0:T(8,128)(2,1)} %get-tuple-element.20.refs_1_, ...), custom_call_target="tpu_custom_call" | custom-call | tf_op jit(solution)/shard_map/pallas_call | solution.py:759

commit v4 on v3

--- a/solution.py
+++ b/solution.py
@@ -55,15 +55,20 @@
         d2 = (go - gs) & 7
         back2 = jnp.where((d2 > FAR) | ((d2 == FAR) & ((fs & 1) == 1)), 1, 0)
         dist2 = jnp.where(back2 == 1, SIDE - d2, d2)
-        for group, dist in ((sender * 2 + back1, dist1), (owner * 2 + back2, dist2)):
-            start = group * (8 * T)
-            starts.append(start.astype(F32))
-            keys.append((start + (FAR - dist) * T + ln).astype(F32))
+        for group, back, dist in ((sender, back1, dist1), (owner, back2, dist2)):
+            level = FAR + jnp.where(back == 1, dist, -dist)
+            starts.append((16 * group, back))
+            keys.append(((group * 16 + level) * T + ln).astype(F32))
         halves.append((back1, dist1, back2, dist2))
-    starts.append((owner * T).astype(F32))
+    starts.append((16 * owner, 0))
     keys.append((owner * T + dealing).astype(F32))
     stacked = jnp.where(row8 == 0, keys[0], jnp.where(row8 == 1, keys[1], jnp.where(row8 == 2, keys[2], jnp.where(row8 == 3, keys[3], keys[4]))))
     return ln, sender, owner, acc, me_y, me_z, halves, keys, starts, stacked
+
+
+def places_of(found, starts):
+    ranks = [count.astype(jnp.int32) - start for count, (start, _) in zip(found, starts)]
+    return [jnp.where(back == 1, 15 - rank, rank) for rank, (_, back) in zip(ranks, starts)]
 
 
 def finish_tables(ln, sender, owner, acc, me, halves, places):
@@ -118,7 +123,7 @@
         return tuple(
             found[k]
             + jnp.sum(
-                jnp.where((part[:, k : k + 1] >= starts[k]) & (part[:, k : k + 1] < keys[k]), 1.0, 0.0),
+                jnp.where(part[:, k : k + 1] < keys[k], 1.0, 0.0),
                 axis=0,
                 keepdims=True,
             )
@@ -129,7 +134,7 @@
         0, total // chunk, count, tuple(jnp.zeros((1, total), F32) for _ in range(5))
     )
     table_ref[...] = finish_tables(
-        ln, sender, owner, acc, me, halves, [places.astype(jnp.int32) for places in found]
+        ln, sender, owner, acc, me, halves, places_of(found, starts)
     )
     tokens = count_ref.shape[0]
     slot = lax.broadcasted_iota(jnp.int32, (tokens, total), 0) >> 4

time: 117 us -> 115 us (0.983)
  Pallas kernels: 116 us -> 114 us
    pallas_call x1, Pallas kernels: 8.01 us -> 6.63 us  [local(): pl.pallas_call(table_kernel, out_shape=(jax.ShapeDtypeStruct((8, 128), jn...]
where the time goes in v4:
time: 115 us
  Pallas kernels  114 us (99%)
    pallas_call x1, Pallas kernels, local(): pl.pallas_call(functools.partial(layer_kernel, count, SIDE), out_shape=(j...  105 us
    pallas_call x1, Pallas kernels, local(): pl.pallas_call(table_kernel, out_shape=(jax.ShapeDtypeStruct((8, 128), jn...  6.63 us
    pallas_call x1, Pallas kernels, local(): pl.pallas_call(hand_over_kernel, out_shape=tuple((jax.ShapeDtypeStruct(on...  2.33 us

profile of v4, /device:TPU:28, one launch (start us, length us, event | category | flops | bytes accessed | tf_op | source)
XLA Modules:
  0.0 115.0 jit_solution(5394617500719869358)
XLA Ops:
  0.6 6.6 %shard_map.245 = (s32[8,128]{1,0:T(8,128)}, s32[256,1]{1,0:T(8,128)}) custom-call(s32[1,1024]{1,0:T(1,128)} %bitcast.18, s32[1,1024]{1,0:T(1,128)} %bitcast.19, s32[1,1024]{1,0:T(1,128)} %bitcast.20), custom_call_target="tpu_custom_call" | custom-call | tf_op jit(solution)/shard_map/pallas_call | solution.py:694
  7.3 105.4 %shard_map.246 = (bf16[192,256]{1,0:T(8,128)(2,1)}, bf16[403,256]{1,0:T(8,128)(2,1)}, bf16[16,192,128]{2,1,0:T(8,128)(2,1)}, bf16[3,16,192]{2,1,0:T(8,128)(2,1)}, bf16[3,16,256]{2,1,0:T(8,128)(2,1)}) custom-call(s32[8,128]{1,0:T(8,128)} %get-tuple-element.17.table_ref, f32[3]{0:T(128)} %bias_ref.1, f32[3]{0:T(128)} %decay_ref.1, f32[3]{0:T(128)} %skip_ref.1, ...), custom_call_target="tpu_custom_call" | custom-call | flops 4000000000 | bytes 100000000 | tf_op jit(solution)/shard_map/pallas_call | solution.py:728
  112.7 2.3 %shard_map.247 = (bf16[192,256]{1,0:T(8,128)(2,1)}, bf16[403,256]{1,0:T(8,128)(2,1)}, bf16[16,192,128]{2,1,0:T(8,128)(2,1)}, bf16[3,16,192]{2,1,0:T(8,128)(2,1)}, bf16[3,16,256]{2,1,0:T(8,128)(2,1)}) custom-call(bf16[192,256]{1,0:T(8,128)(2,1)} %get-tuple-element.19.refs_0_, bf16[403,256]{1,0:T(8,128)(2,1)} %get-tuple-element.20.refs_1_, ...), custom_call_target="tpu_custom_call" | custom-call | tf_op jit(solution)/shard_map/pallas_call | solution.py:764

commit v5 on v4

--- a/solution.py
+++ b/solution.py
@@ -549,20 +549,21 @@
     states.after(1)
 
     crossing = lax.dot_general(
-        c_part, b_part, (((1,), (1,)), ((), ())), precision=HIGHEST, preferred_element_type=F32
+        c_part.astype(BF16), b_part.astype(BF16), (((1,), (1,)), ((), ())), preferred_element_type=F32
     )
     direct = jnp.zeros((tokens, block), F32)
     for head in range(3):
         column = cumul[:, head : head + 1]
         gap = jnp.where(tri, column - to_row(column), 0.0)
         mixing = jnp.where(tri, jnp.exp(gap), 0.0) * to_row(steps[:, head : head + 1]) * crossing
-        direct = direct + fdot(mixing, jnp.where((lane >> 6) == head, conv_i, 0.0))
+        direct = direct + bdot(
+            mixing.astype(BF16), jnp.where((lane >> 6) == head, conv_i, 0.0).astype(BF16)
+        )
     updates.first(1)
     carried = lax.dot_general(
-        c_part.reshape(requests, length, 128),
-        start_ref[...].astype(F32),
+        c_part.astype(BF16).reshape(requests, length, 128),
+        start_ref[...],
         (((2,), (2,)), ((0,), (0,))),
-        precision=HIGHEST,
         preferred_element_type=F32,
     ).reshape(tokens, block)
     outputs = carried * spread(jnp.exp(cumul)) + direct + scalars(skip_ref, lane, 64) * conv_i

time: 115 us -> 115 us (level)
  the two profiles are of different devices: /device:TPU:28 before, /device:TPU:24 now
where the time goes in v5:
time: 115 us
  Pallas kernels  114 us (99%)
    pallas_call x1, Pallas kernels, local(): pl.pallas_call(functools.partial(layer_kernel, count, SIDE), out_shape=(j...  105 us
    pallas_call x1, Pallas kernels, local(): pl.pallas_call(table_kernel, out_shape=(jax.ShapeDtypeStruct((8, 128), jn...  6.63 us
    pallas_call x1, Pallas kernels, local(): pl.pallas_call(hand_over_kernel, out_shape=tuple((jax.ShapeDtypeStruct(on...  2.33 us

profile of v5, /device:TPU:24, one launch (start us, length us, event | category | flops | bytes accessed | tf_op | source)
XLA Modules:
  0.0 114.7 jit_solution(8208187268804191002)
XLA Ops:
  0.6 6.6 %shard_map.245 = (s32[8,128]{1,0:T(8,128)}, s32[256,1]{1,0:T(8,128)}) custom-call(s32[1,1024]{1,0:T(1,128)} %bitcast.18, s32[1,1024]{1,0:T(1,128)} %bitcast.19, s32[1,1024]{1,0:T(1,128)} %bitcast.20), custom_call_target="tpu_custom_call" | custom-call | tf_op jit(solution)/shard_map/pallas_call | solution.py:695
  7.3 105.1 %shard_map.246 = (bf16[192,256]{1,0:T(8,128)(2,1)}, bf16[403,256]{1,0:T(8,128)(2,1)}, bf16[16,192,128]{2,1,0:T(8,128)(2,1)}, bf16[3,16,192]{2,1,0:T(8,128)(2,1)}, bf16[3,16,256]{2,1,0:T(8,128)(2,1)}) custom-call(s32[8,128]{1,0:T(8,128)} %get-tuple-element.17.table_ref, f32[3]{0:T(128)} %bias_ref.1, f32[3]{0:T(128)} %decay_ref.1, f32[3]{0:T(128)} %skip_ref.1, ...), custom_call_target="tpu_custom_call" | custom-call | flops 4000000000 | bytes 100000000 | tf_op jit(solution)/shard_map/pallas_call | solution.py:729
  112.4 2.3 %shard_map.247 = (bf16[192,256]{1,0:T(8,128)(2,1)}, bf16[403,256]{1,0:T(8,128)(2,1)}, bf16[16,192,128]{2,1,0:T(8,128)(2,1)}, bf16[3,16,192]{2,1,0:T(8,128)(2,1)}, bf16[3,16,256]{2,1,0:T(8,128)(2,1)}) custom-call(bf16[192,256]{1,0:T(8,128)(2,1)} %get-tuple-element.19.refs_0_, bf16[403,256]{1,0:T(8,128)(2,1)} %get-tuple-element.20.refs_1_, ...), custom_call_target="tpu_custom_call" | custom-call | tf_op jit(solution)/shard_map/pallas_call | solution.py:765
